TPU v7x, 128 devices: a whole 4x4x4 slice. The times are simulated.
128 devices in a mesh: span: 16 (over y, x_hi, core), tok: 8 (over x_lo, z).
Axes of the slice: x: 4 (x_hi: 2, x_lo: 2; x = x_hi * 2 + x_lo), y: 4, z: 4, core: 2. Of those that a mesh axis runs over, the one named last changes fastest.
Arguments:
- queries: bfloat16 [16, 512, 3072], P('span', 'tok'), may hold values from -9 to 9
- keys: bfloat16 [16, 512, 3072], P('span', 'tok'), may hold values from -9 to 9
- values: bfloat16 [16, 512, 3072], P('span', 'tok'), may hold values from -6 to 6
- levels: int32 [16], P('span'), may hold values from 0 to 15
- retiring: int32 [1], replicated, may hold values from 0 to 15
- block_mask: int32 [16, 16], P('span'), may hold values 0 or 1
- gates: float32 [16, 3072], replicated, may hold values from 0.5 to 2
Outputs:
- attended: bfloat16 [16, 512, 3072], P('span', 'tok')
All inputs are finite; a program needn't handle non-finite values. No bound on the sum of `block_mask` on one device may be relied on, other than what follows from the above.
Results may differ from a plain program's by a relative error of at most 0.0085.
Values may be sent and summed in bfloat16 or wider, within the bound.
No kernel may reach another device: no remote copies, remote signals or barrier semaphores. Data moves between devices by JAX's collectives and lax.ppermute only.
A program may use at most 128 MiB of HBM per device.

v0:
```python
import functools

import jax
import jax.numpy as jnp
from jax import lax
from jax.experimental import pallas as pl
from jax.experimental.pallas import tpu as pltpu
from jax.sharding import PartitionSpec as P


HEAD_DIM = 128
SPANS = 16
ROWS = 64
GROUP = 8
HEADS_DEV = 3
WIDTH = HEADS_DEV * HEAD_DIM
RING = 4
SET = GROUP * ROWS
META = 32
PARTS = ((0,), (1, 2))
TILE = 2 * ROWS
TILES = 16
STEP = 4
SUB = 2
LOG2E = 1.4426950408889634


BOTH = ("span", "tok")
VMEM = pl.BlockSpec(memory_space=pltpu.VMEM)
SMEM = pl.BlockSpec(memory_space=pltpu.SMEM)


def device_at(x, y, z, core):
    return (y * 4 + (x // 2) * 2 + core) * 8 + (x % 2) * 4 + z


def moved(array, dx=0, dy=0, dz=0, core=0, swap=0):
    pairs = []
    for x in range(4):
        for y in range(4):
            for z in range(4):
                for c in range(2):
                    mx, mz = (dz, dx) if swap and c else (dx, dz)
                    there = device_at((x + mx) % 4, (y + dy) % 4, (z + mz) % 4, c ^ core)
                    pairs.append((device_at(x, y, z, c), there))
    return lax.ppermute(array, BOTH, pairs)


def call(kernel, shapes, specs, scratch=()):
    return pl.pallas_call(
        kernel,
        out_shape=shapes,
        in_specs=specs,
        out_specs=jax.tree.map(lambda unused: VMEM, shapes),
        scratch_shapes=scratch,
    )


def shape(rows, columns, dtype=jnp.bfloat16):
    return jax.ShapeDtypeStruct((rows, columns), dtype)


def pack_kernel(at_ref, q_ref, k_ref, v_ref, meta_ref, *out_refs):
    for j in range(GROUP):
        columns = pl.ds(pl.multiple_of(at_ref[j] * WIDTH, HEAD_DIM), WIDTH)
        for i, ref in enumerate((q_ref, k_ref, v_ref)):
            out_refs[j][i * ROWS : (i + 1) * ROWS, :] = ref[:, columns]
        out_refs[j][3 * ROWS :, :] = meta_ref[...]


def spread_kernel(*refs):
    in_refs, out_refs = refs[:GROUP], refs[GROUP:]
    for j in range(GROUP):
        ref = in_refs[j]
        for p, part in enumerate(PARTS):
            q_ref, kv_ref = out_refs[2 * p], out_refs[2 * p + 1]
            for i, h in enumerate(part):
                columns = slice(h * HEAD_DIM, (h + 1) * HEAD_DIM)
                q_ref[i * SET + j * ROWS : i * SET + (j + 1) * ROWS, :] = ref[0:ROWS, columns]
                for t in range(2):
                    base = (2 * i + t) * SET + j * ROWS
                    kv_ref[base : base + ROWS, :] = ref[(t + 1) * ROWS : (t + 2) * ROWS, columns]
        row = ref[3 * ROWS : 3 * ROWS + 16, 0:HEAD_DIM].astype(jnp.float32)
        out_refs[-1][j : j + 1, :] = row[0:1]


def together_in(count):
    return 2 if count == 1 else 1


def attend_kernel(count, table_ref, *refs):
    together = together_in(count)
    q_refs, kv_refs = refs[:RING], refs[RING : 2 * RING]
    out_refs = refs[2 * RING : 3 * RING]
    q_all, k_all, v_all, o_all, v_turned, score_ref, lse_ref, sems = refs[3 * RING :]
    factor = jnp.float32(HEAD_DIM ** (-0.5) * LOG2E)

    def rows_of(ref, h, i):
        return ref[h, i // 2, pl.ds(i % 2 * 2, 2)].reshape(TILE, HEAD_DIM)

    limits = TILES * TILES
    q_place = [table_ref[limits + TILES + d] for d in range(RING)]
    k_place = [table_ref[limits + TILES + RING + d] for d in range(RING)]
    copies = []
    for h in range(count):
        for d in range(RING):
            for n, (source, target, place) in enumerate(
                (
                    (q_refs[d].at[h], q_all, q_place[d]),
                    (kv_refs[d].at[h, 0], k_all, k_place[d]),
                    (kv_refs[d].at[h, 1], v_all, k_place[d]),
                )
            ):
                copy = pltpu.make_async_copy(
                    source, target.at[h, :, place], sems.at[(h * RING + d) * 3 + n]
                )
                copy.start()
                copies.append(copy)
    for copy in copies:
        copy.wait()
    for h in range(count):
        for i in range(TILES):
            rows = slice(i * TILE, (i + 1) * TILE)
            v_turned[h, :, rows] = rows_of(v_all, h, i).T

    def tiles(first, unused):
        picks = [first * together + t for t in range(together)]
        seen = [table_ref[limits + i] for i in picks]
        trips = functools.reduce(jnp.maximum, seen)
        chains = [(t, h) for t in range(together) for h in range(count)]
        starts = [pl.multiple_of(i * TILE, TILE) for i in picks]

        def fill(g):
            for c, (t, h) in enumerate(chains):
                rows = [rows_of(k_all, h, place(t, g, u)) for u in range(STEP)]
                score_ref[c] = lax.dot_general(
                    jnp.concatenate(rows, axis=0),
                    rows_of(q_all, h, picks[t]),
                    (((1,), (1,)), ((), ())),
                    preferred_element_type=jnp.float32,
                )

        def place(t, g, u):
            return table_ref[picks[t] * TILES + g * STEP + u]

        fill(0)

        def step(g, carry):
            parts = [range(at, at + SUB) for at in range(0, STEP, SUB)]
            scores = [score_ref[c] for c in range(len(chains))]
            fill(jnp.minimum(g + 1, TILES // STEP - 1))
            result = list(carry)
            for part in parts:
                for c, (t, h) in enumerate(chains):
                    top, total, acc = result[c]
                    score = scores[c][part[0] * TILE : (part[-1] + 1) * TILE]
                    blocks = []
                    for n, u in enumerate(part):
                        block = score[n * TILE : (n + 1) * TILE]
                        blocks.append(jnp.where(g * STEP + u < seen[t], block, -1e30))
                    largest = functools.reduce(jnp.maximum, blocks)
                    new_top = jnp.maximum(top, jnp.max(largest, axis=0, keepdims=True))
                    shrink = jnp.exp2((top - new_top) * factor)
                    weights = [jnp.exp2((block - new_top) * factor) for block in blocks]
                    added = functools.reduce(jnp.add, weights).reshape(TILE // 8, 8, TILE)
                    total = total * shrink + jnp.sum(added, axis=0)
                    weight = jnp.concatenate([w.astype(jnp.bfloat16) for w in weights], axis=0)
                    columns = [v_turned[h, :, pl.ds(pl.multiple_of(place(t, g, u) * TILE, TILE), TILE)] for u in part]
                    acc = acc * shrink + jnp.dot(
                        jnp.concatenate(columns, axis=1),
                        weight,
                        preferred_element_type=jnp.float32,
                    )
                    result[c] = (new_top, total, acc)
            return result

        empty = (
            jnp.full((1, TILE), -1e30, jnp.float32),
            jnp.zeros((8, TILE), jnp.float32),
            jnp.zeros((HEAD_DIM, TILE), jnp.float32),
        )
        final = lax.fori_loop(0, (trips + STEP - 1) // STEP, step, [empty] * len(chains))
        for (t, h), (top, total, acc) in zip(chains, final):
            total = jnp.sum(total, axis=0, keepdims=True)
            total = jnp.where(total > 0.0, total, 1.0)
            o_all[h, pl.ds(starts[t], TILE), :] = (acc * (1.0 / total)).T.astype(jnp.bfloat16)
            lse_ref[h, picks[t] % 2, pl.ds(picks[t] // 2, 1), :] = top * factor + jnp.log2(total)
        return unused

    lax.fori_loop(0, TILES // together, tiles, 0)
    for h in range(count):
        for d in range(RING):
            base = h * (SET + META)
            for j in range(GROUP):
                at = pl.multiple_of(j * RING * ROWS + q_place[d] * ROWS, ROWS)
                out_refs[d][base + j * ROWS : base + (j + 1) * ROWS, :] = o_all[
                    h, pl.ds(at, ROWS), :
                ]
            value = lse_ref[h, q_place[d] // 2]
            high = value.astype(jnp.bfloat16).astype(jnp.float32)
            middle = (value - high).astype(jnp.bfloat16).astype(jnp.float32)
            low = value - high - middle
            out_refs[d][base + SET : base + SET + META, :] = jnp.concatenate(
                [high, middle, low, jnp.zeros_like(low)], axis=0
            ).astype(jnp.bfloat16)


def attend(count, table, q, kv):
    q = [piece.reshape(count, GROUP, ROWS, HEAD_DIM) for piece in q]
    kv = [piece.reshape(count, 2, GROUP, ROWS, HEAD_DIM) for piece in kv]
    pieces = pltpu.VMEM((count, GROUP, RING, ROWS, HEAD_DIM), jnp.bfloat16)
    return call(
        functools.partial(attend_kernel, count),
        [shape(count * (SET + META), HEAD_DIM)] * RING,
        [SMEM] + [pl.BlockSpec(memory_space=pl.ANY)] * (2 * RING),
        [pieces] * 3
        + [
            pltpu.VMEM((count, RING * SET, HEAD_DIM), jnp.bfloat16),
            pltpu.VMEM((count, HEAD_DIM, RING * SET), jnp.bfloat16),
            pltpu.VMEM((count * together_in(count), STEP * TILE, TILE), jnp.float32),
            pltpu.VMEM((count, 2, GROUP, HEAD_DIM), jnp.float32),
            pltpu.SemaphoreType.DMA((count * RING * 3,)),
        ],
    )(table, *q, *kv)


def combine_kernel(table_ref, *refs):
    out_refs = refs[-GROUP:]
    shift = table_ref[TILES * TILES + TILES] % 2 * ROWS
    lanes = lax.broadcasted_iota(jnp.int32, (ROWS, HEAD_DIM), 1)
    eye = lanes == lax.broadcasted_iota(jnp.int32, (ROWS, HEAD_DIM), 0) + shift
    for p, part in enumerate(PARTS):
        pieces = refs[p * RING : (p + 1) * RING]
        for i, h in enumerate(part):
            base = i * (SET + META)
            lse = []
            for ref in pieces:
                coded = ref[base + SET : base + SET + META, :].astype(jnp.float32)
                lse.append(coded[0:8] + coded[8:16] + coded[16:24])
            top = functools.reduce(jnp.maximum, lse)
            shares = [jnp.exp2(value - top) for value in lse]
            total = functools.reduce(jnp.add, shares)
            shares = [value / total for value in shares]
            for j in range(GROUP):
                mixed = jnp.zeros((ROWS, HEAD_DIM), jnp.float32)
                for ref, share in zip(pieces, shares):
                    column = jnp.sum(jnp.where(eye, share[j : j + 1], 0.0), axis=1, keepdims=True)
                    rows = ref[base + j * ROWS : base + (j + 1) * ROWS, :]
                    mixed = mixed + column * rows.astype(jnp.float32)
                out_refs[j][:, h * HEAD_DIM : (h + 1) * HEAD_DIM] = mixed.astype(jnp.bfloat16)


def finish_kernel(at_ref, level_ref, gates_ref, *refs):
    out_ref = refs[-1]
    for j in range(GROUP):
        columns = pl.ds(pl.multiple_of(at_ref[j] * WIDTH, HEAD_DIM), WIDTH)
        gate = gates_ref[pl.ds(level_ref[0], 1), columns]
        out_ref[:, columns] = (refs[j][...].astype(jnp.float32) * gate).astype(jnp.bfloat16)


def see_table(q_slots, k_slots, retiring, mask, places):
    names = jnp.arange(TILES, dtype=jnp.int32)
    q_order = (q_slots - retiring[0]) % SPANS
    k_order = (k_slots - retiring[0]) % SPANS
    slots = jnp.arange(SPANS, dtype=jnp.int32)
    picked = (k_slots[:, None] == slots[None, :]).astype(jnp.float32)
    masked = jnp.sum(mask[:, None, :SPANS] * picked[None], axis=-1) > 0.5
    older = k_order[None, :] < q_order[:, None]
    same = k_slots[None, :] == q_slots[:, None]
    sees = same | masked & older
    before = names[None, :] < names[:, None]
    rank = jnp.sum((sees[:, None, :] & before[None]).astype(jnp.int32), axis=-1)
    chosen = sees[:, None, :] & (rank[:, None, :] == names[None, :, None])
    listed = jnp.sum(jnp.where(chosen, names[None, None, :], 0), axis=-1)
    counts = jnp.sum(sees.astype(jnp.int32), axis=-1)
    return jnp.concatenate([listed.reshape(-1), counts, places])


def local(queries, keys, values, levels, retiring, block_mask, gates):
    span = lax.axis_index("span").astype(jnp.int32)
    token = lax.axis_index("tok").astype(jnp.int32)
    y, half, core = span // 4, span // 2 % 2, span % 2
    x, z = half * 2 + token // RING, token % RING
    hop = jnp.arange(GROUP, dtype=jnp.int32)
    target = (y + hop // 2) % 4 * 2 + (core ^ hop % 2)
    hops = [dict(dy=j // 2, core=j % 2) for j in range(GROUP)]
    backs = [dict(dy=-(j // 2), core=j % 2) for j in range(GROUP)]

    meta = jnp.pad(block_mask.astype(jnp.bfloat16), ((0, 15), (0, WIDTH - SPANS)))
    packed = call(
        pack_kernel,
        [shape(3 * ROWS + 16, WIDTH)] * GROUP,
        [SMEM, VMEM, VMEM, VMEM, VMEM],
    )(target, queries[0], keys[0], values[0], meta)
    shared = [packed[0]] + [moved(packed[j], **hops[j]) for j in range(1, GROUP)]

    shapes = []
    for part in PARTS:
        shapes += [shape(len(part) * SET, HEAD_DIM), shape(len(part) * 2 * SET, HEAD_DIM)]
    spread = call(
        spread_kernel, shapes + [shape(GROUP, HEAD_DIM, jnp.float32)], [VMEM] * GROUP
    )(*shared)

    tile = jnp.arange(TILES, dtype=jnp.int32)
    base = (y - tile // 4) % 4 * 4 + (core ^ tile // 2 % 2)
    wide_slots, near_slots = base + 2 * (tile % 2), base + 2 * half
    near_mask = jnp.repeat(spread[-1], 2, axis=0)
    far_mask = jnp.repeat(moved(spread[-1], dx=2), 2, axis=0)
    wide_mask = jnp.where((tile % 2 == half)[:, None], near_mask, far_mask)
    first = core == 0
    ring = jnp.arange(RING, dtype=jnp.int32)
    table = see_table(
        jnp.where(first, wide_slots, near_slots),
        jnp.where(first, near_slots, wide_slots),
        retiring,
        jnp.where(first, wide_mask, near_mask),
        jnp.concatenate(
            [(jnp.where(first, x, z) - ring) % RING, (jnp.where(first, z, x) - ring) % RING]
        ),
    )

    pieces = []
    for p, part in enumerate(PARTS):
        own_q, own_kv = spread[2 * p], spread[2 * p + 1]
        q, kv = [own_q], [own_kv]
        for d in range(1, RING):
            kv.append(moved(own_kv, dz=d, swap=1))
        for d in range(1, RING):
            q.append(moved(own_q, dx=d, swap=1))
        parts = attend(len(part), table, q, kv)
        pieces.append(parts[0])
        for d in range(1, RING):
            pieces.append(moved(parts[d], dx=-d, swap=1))

    mixed = call(
        combine_kernel, [shape(ROWS, WIDTH)] * GROUP, [SMEM] + [VMEM] * len(pieces)
    )(table, *pieces)
    returned = [mixed[0]] + [moved(mixed[j], **backs[j]) for j in range(1, GROUP)]
    result = call(finish_kernel, shape(ROWS, GROUP * WIDTH), [SMEM, SMEM] + [VMEM] * (GROUP + 1))(
        target, levels, gates, *returned
    )
    return result[None]


def solution(mesh):
    return jax.shard_map(
        local,
        mesh=mesh,
        in_specs=(
            P("span", "tok", None),
            P("span", "tok", None),
            P("span", "tok", None),
            P("span"),
            P(),
            P("span", None),
            P(),
        ),
        out_specs=P("span", "tok", None),
        check_vma=False,
    )
```

profile of v0, /device:TPU:1, one launch (start us, length us, event | category | flops | bytes accessed | tf_op | source)
XLA Modules:
  0.0 129.1 jit_solution(12849554404433149931)
XLA Ops:
  1.8 2.4 %shard_map.73 = (bf16[208,384]{1,0:T(8,128)(2,1)}, bf16[208,384]{1,0:T(8,128)(2,1)}, bf16[208,384]{1,0:T(8,128)(2,1)}, bf16[208,384]{1,0:T(8,128)(2,1)}, bf16[20...) custom-call(s32[8]{0:T(128)} %fusion.3.at_ref, ...), custom_call_target="tpu_custom_call" | custom-call | tf_op jit(solution)/shard_map/pallas_call | solution.py:290
  4.2 1.4 %collective-permute-start = (bf16[208,384]{1,0:T(8,128)(2,1)}, bf16[208,384]{1,0:T(8,128)(2,1)S(1)}, u32[]{:S(2)}, u32[]{:S(2)}) collective-permute-start(bf16[208,384]{1,0:T(8,128)(2,1)} %get-tuple-element.35), channel_id=1, source_target_pairs={{0,8},{8,0},{1,9},{9,1},{2,10},{10,2},{3,11},{11,3},{32,40},{40,32... | collective-permute-start | bytes 479240 | tf_op jit(solution)/shard_map/ppermute | solution.py:46
  5.6 1.4 %collective-permute-start.1 = (bf16[208,384]{1,0:T(8,128)(2,1)}, bf16[208,384]{1,0:T(8,128)(2,1)S(1)}, u32[]{:S(2)}, u32[]{:S(2)}) collective-permute-start(bf16[208,384]{1,0:T(8,128)(2,1)} %get-tuple-element.36), channel_id=1, source_target_pairs={{0,32},{8,40},{1,33},{9,41},{2,34},{10,42},{3,35},{11,43},{32,64},... | collective-permute-start | bytes 479240 | tf_op jit(solution)/shard_map/ppermute | solution.py:46
  7.0 1.5 %collective-permute-start.2 = (bf16[208,384]{1,0:T(8,128)(2,1)}, bf16[208,384]{1,0:T(8,128)(2,1)S(1)}, u32[]{:S(2)}, u32[]{:S(2)}) collective-permute-start(bf16[208,384]{1,0:T(8,128)(2,1)} %get-tuple-element.37), channel_id=1, source_target_pairs={{0,40},{8,32},{1,41},{9,33},{2,42},{10,34},{3,43},{11,35},{32,72},... | collective-permute-start | bytes 479240 | tf_op jit(solution)/shard_map/ppermute | solution.py:46
  9.6 2.2 %collective-permute-start.4 = (bf16[208,384]{1,0:T(8,128)(2,1)}, bf16[208,384]{1,0:T(8,128)(2,1)S(1)}, u32[]{:S(2)}, u32[]{:S(2)}) collective-permute-start(bf16[208,384]{1,0:T(8,128)(2,1)} %get-tuple-element.39), channel_id=1, source_target_pairs={{0,72},{8,64},{1,73},{9,65},{2,74},{10,66},{3,75},{11,67},{32,104}... | collective-permute-start | bytes 479240 | tf_op jit(solution)/shard_map/ppermute | solution.py:46
  12.6 1.4 %collective-permute-start.5 = (bf16[208,384]{1,0:T(8,128)(2,1)}, bf16[208,384]{1,0:T(8,128)(2,1)S(1)}, u32[]{:S(2)}, u32[]{:S(2)}) collective-permute-start(bf16[208,384]{1,0:T(8,128)(2,1)} %get-tuple-element.40), channel_id=1, source_target_pairs={{0,96},{8,104},{1,97},{9,105},{2,98},{10,106},{3,99},{11,107},{32,... | collective-permute-start | bytes 479240 | tf_op jit(solution)/shard_map/ppermute | solution.py:46
  14.0 1.5 %collective-permute-start.6 = (bf16[208,384]{1,0:T(8,128)(2,1)}, bf16[208,384]{1,0:T(8,128)(2,1)S(1)}, u32[]{:S(2)}, u32[]{:S(2)}) collective-permute-start(bf16[208,384]{1,0:T(8,128)(2,1)} %get-tuple-element.41), channel_id=1, source_target_pairs={{0,104},{8,96},{1,105},{9,97},{2,106},{10,98},{3,107},{11,99},{32,... | collective-permute-start | bytes 479240 | tf_op jit(solution)/shard_map/ppermute | solution.py:46
  16.4 4.4 %collective-permute-done.3.refs_4_ = bf16[208,384]{1,0:T(8,128)(2,1)S(1)} collective-permute-done((bf16[208,384]{1,0:T(8,128)(2,1)}, bf16[208,384]{1,0:T(8,128)(2,1)S(1)}, u32[]{:S(2)}, u32[]{:S(2)}) %collective-permute-start.3) | collective-permute-done | bytes 159776 | tf_op jit(solution)/shard_map/ppermute | solution.py:46
  20.8 3.6 %collective-permute-done.4.refs_5_ = bf16[208,384]{1,0:T(8,128)(2,1)S(1)} collective-permute-done((bf16[208,384]{1,0:T(8,128)(2,1)}, bf16[208,384]{1,0:T(8,128)(2,1)S(1)}, u32[]{:S(2)}, u32[]{:S(2)}) %collective-permute-start.4) | collective-permute-done | bytes 159776 | tf_op jit(solution)/shard_map/ppermute | solution.py:46
  26.0 2.6 %shard_map.74 = (bf16[512,128]{1,0:T(8,128)(2,1)}, bf16[1024,128]{1,0:T(8,128)(2,1)}, bf16[1024,128]{1,0:T(8,128)(2,1)}, bf16[2048,128]{1,0:T(8,128)(2,1)}, f32[8,128]{1,0:T(8,128)}) custom-call(bf16[208,384]{1,0:T(8,128)(2,1)} %get-tuple-element.34.refs_0_, bf16[208,384]{1,0:T(8,128)(2,1)} %copy-done.12, bf16[208,384]{1,0:T(8,128)(2,1)} %copy-done.13, ...), custom_call_target="tpu_custom_call" | custom-call | tf_op jit(solution)/shard_map/pallas_call | solution.py:300
  28.6 2.7 %collective-permute-start.7 = (f32[8,128]{1,0:T(8,128)}, f32[8,128]{1,0:T(8,128)S(1)}, u32[]{:S(2)}, u32[]{:S(2)}) collective-permute-start(f32[8,128]{1,0:T(8,128)} %get-tuple-element.42), channel_id=1, source_target_pairs={{0,16},{8,24},{1,17},{9,25},{2,18},{10,26},{3,19},{11,27},{32,48},... | collective-permute-start | bytes 12296 | tf_op jit(solution)/shard_map/ppermute | solution.py:46
  31.3 1.6 %collective-permute-start.8 = (bf16[512,128]{1,0:T(8,128)(2,1)}, bf16[512,128]{1,0:T(8,128)(2,1)S(1)}, u32[]{:S(2)}, u32[]{:S(2)}) collective-permute-start(bf16[512,128]{1,0:T(8,128)(2,1)} %get-tuple-element.43), channel_id=1, source_target_pairs={{0,4},{8,9},{1,5},{9,10},{2,6},{10,11},{3,7},{11,8},{32,36},{40,41... | collective-permute-start | bytes 393224 | tf_op jit(solution)/shard_map/ppermute | solution.py:46
  33.0 3.3 %collective-permute-start.9 = (bf16[512,128]{1,0:T(8,128)(2,1)}, bf16[512,128]{1,0:T(8,128)(2,1)S(1)}, u32[]{:S(2)}, u32[]{:S(2)}) collective-permute-start(bf16[512,128]{1,0:T(8,128)(2,1)} %get-tuple-element.43), channel_id=1, source_target_pairs={{0,16},{8,10},{1,17},{9,11},{2,18},{10,8},{3,19},{11,9},{32,48},{4... | collective-permute-start | bytes 393224 | tf_op jit(solution)/shard_map/ppermute | solution.py:46
  38.5 1.4 %collective-permute-start.12 = (bf16[1024,128]{1,0:T(8,128)(2,1)}, bf16[1024,128]{1,0:T(8,128)(2,1)S(1)}, u32[]{:S(2)}, u32[]{:S(2)}) collective-permute-start(bf16[1024,128]{1,0:T(8,128)(2,1)} %get-tuple-element.44), channel_id=1, source_target_pairs={{0,2},{8,24},{1,3},{9,25},{2,0},{10,26},{3,1},{11,27},{32,34},{40,... | collective-permute-start | bytes 786440 | tf_op jit(solution)/shard_map/ppermute | solution.py:46
  41.9 4.3 %collective-permute-done.17 = bf16[1024,128]{1,0:T(8,128)(2,1)S(1)} collective-permute-done((bf16[1024,128]{1,0:T(8,128)(2,1)}, bf16[1024,128]{1,0:T(8,128)(2,1)S(1)}, u32[]{:S(2)}, u32[]{:S(2)}) %collective-permute-start.17) | collective-permute-done | bytes 262176 | tf_op jit(solution)/shard_map/ppermute | solution.py:46
  46.2 1.8 %collective-permute-done.11 = bf16[1024,128]{1,0:T(8,128)(2,1)S(1)} collective-permute-done((bf16[1024,128]{1,0:T(8,128)(2,1)}, bf16[1024,128]{1,0:T(8,128)(2,1)S(1)}, u32[]{:S(2)}, u32[]{:S(2)}) %collective-permute-start.11) | collective-permute-done | bytes 262176 | tf_op jit(solution)/shard_map/ppermute | solution.py:46
  48.2 2.2 %collective-permute-start.18 = (bf16[1024,128]{1,0:T(8,128)(2,1)}, bf16[1024,128]{1,0:T(8,128)(2,1)S(1)}, u32[]{:S(2)}, u32[]{:S(2)}) collective-permute-start(bf16[1024,128]{1,0:T(8,128)(2,1)} %get-tuple-element.49), channel_id=1, source_target_pairs={{0,16},{8,10},{1,17},{9,11},{2,18},{10,8},{3,19},{11,9},{32,48},{4... | collective-permute-start | bytes 786440 | tf_op jit(solution)/shard_map/ppermute | solution.py:46
  50.4 1.8 %collective-permute-start.19 = (bf16[1024,128]{1,0:T(8,128)(2,1)}, bf16[1024,128]{1,0:T(8,128)(2,1)S(1)}, u32[]{:S(2)}, u32[]{:S(2)}) collective-permute-start(bf16[1024,128]{1,0:T(8,128)(2,1)} %get-tuple-element.49), channel_id=1, source_target_pairs={{0,20},{8,11},{1,21},{9,8},{2,22},{10,9},{3,23},{11,10},{32,52},{4... | collective-permute-start | bytes 786440 | tf_op jit(solution)/shard_map/ppermute | solution.py:46
  54.3 12.0 %shard_map.75 = (bf16[544,128]{1,0:T(8,128)(2,1)}, bf16[544,128]{1,0:T(8,128)(2,1)}, bf16[544,128]{1,0:T(8,128)(2,1)}, bf16[544,128]{1,0:T(8,128)(2,1)}) custom-call(s32[280]{0:T(512)} %pad_add_fusion.table_ref, bf16[1,8,64,128]{3,2,1,0:T(8,128)(2,1)} %bitcast.39, bf16[1,8,64,128]{3,2,1,0:T(8,128)(2,1)} %bitcast.40, bf16[1,8,64,128]{3,2,1,0:T(8,128)(2,1)} %bitcast.41, ...), custom_call_target="tpu_custom_call" | custom-call | tf_op jit(solution)/shard_map/pallas_call | solution.py:212
  67.7 21.0 %shard_map.76 = (bf16[1088,128]{1,0:T(8,128)(2,1)}, bf16[1088,128]{1,0:T(8,128)(2,1)}, bf16[1088,128]{1,0:T(8,128)(2,1)}, bf16[1088,128]{1,0:T(8,128)(2,1)}) custom-call(s32[280]{0:T(512)} %pad_add_fusion.table_ref, bf16[2,8,64,128]{3,2,1,0:T(8,128)(2,1)} %bitcast.35, bf16[2,8,64,128]{3,2,1,0:T(8,128)(2,1)} %bitcast.36, bf16[2,8,64,128]{3,2,1,0:T(8,128)(2,1)} %bitcast.37, ...), custom_call_target="tpu_custom_call" | custom-call | tf_op jit(solution)/shard_map/pallas_call | solution.py:212
  88.7 2.6 %collective-permute-start.23 = (bf16[1088,128]{1,0:T(8,128)(2,1)}, bf16[1088,128]{1,0:T(8,128)(2,1)S(1)}, u32[]{:S(2)}, u32[]{:S(2)}) collective-permute-start(bf16[1088,128]{1,0:T(8,128)(2,1)} %get-tuple-element.52), channel_id=1, source_target_pairs={{0,20},{8,11},{1,21},{9,8},{2,22},{10,9},{3,23},{11,10},{32,52},{4... | collective-permute-start | bytes 835592 | tf_op jit(solution)/shard_map/ppermute | solution.py:46
  92.0 2.3 %collective-permute-start.15 = (bf16[544,128]{1,0:T(8,128)(2,1)S(1)}, bf16[544,128]{1,0:T(8,128)(2,1)S(1)}, u32[]{:S(2)}, u32[]{:S(2)}) collective-permute-start(bf16[544,128]{1,0:T(8,128)(2,1)S(1)} %copy-done.36), channel_id=1, source_target_pairs={{0,16},{8,10},{1,17},{9,11},{2,18},{10,8},{3,19},{11,9},{32,48},{4... | collective-permute-start | bytes 417800 | tf_op jit(solution)/shard_map/ppermute | solution.py:46
  95.5 7.6 %collective-permute-done.15.refs_2_ = bf16[544,128]{1,0:T(8,128)(2,1)S(1)} collective-permute-done((bf16[544,128]{1,0:T(8,128)(2,1)S(1)}, bf16[544,128]{1,0:T(8,128)(2,1)S(1)}, u32[]{:S(2)}, u32[]{:S(2)}) %collective-permute-start.15) | collective-permute-done | bytes 139296 | tf_op jit(solution)/shard_map/ppermute | solution.py:46
  103.1 1.6 %collective-permute-done.16.refs_3_ = bf16[544,128]{1,0:T(8,128)(2,1)S(1)} collective-permute-done((bf16[544,128]{1,0:T(8,128)(2,1)S(1)}, bf16[544,128]{1,0:T(8,128)(2,1)S(1)}, u32[]{:S(2)}, u32[]{:S(2)}) %collective-permute-start.16) | collective-permute-done | bytes 139296 | tf_op jit(solution)/shard_map/ppermute | solution.py:46
  105.7 3.0 %shard_map.77 = (bf16[64,384]{1,0:T(8,128)(2,1)}, bf16[64,384]{1,0:T(8,128)(2,1)}, bf16[64,384]{1,0:T(8,128)(2,1)}, bf16[64,384]{1,0:T(8,128)(2,1)}, bf16[64,384...) custom-call(s32[280]{0:T(512)} %pad_add_fusion.table_ref, ...), custom_call_target="tpu_custom_call" | custom-call | tf_op jit(solution)/shard_map/pallas_call | solution.py:335
  108.6 4.7 %collective-permute-start.26 = (bf16[64,384]{1,0:T(8,128)(2,1)}, bf16[64,384]{1,0:T(8,128)(2,1)S(1)}, u32[]{:S(2)}, u32[]{:S(2)}) collective-permute-start(bf16[64,384]{1,0:T(8,128)(2,1)} %get-tuple-element.56), channel_id=1, source_target_pairs={{0,8},{8,0},{1,9},{9,1},{2,10},{10,2},{3,11},{11,3},{32,40},{40,32... | collective-permute-start | bytes 147464 | tf_op jit(solution)/shard_map/ppermute | solution.py:46
  113.4 3.1 %collective-permute-start.27 = (bf16[64,384]{1,0:T(8,128)(2,1)}, bf16[64,384]{1,0:T(8,128)(2,1)S(1)}, u32[]{:S(2)}, u32[]{:S(2)}) collective-permute-start(bf16[64,384]{1,0:T(8,128)(2,1)} %get-tuple-element.57), channel_id=1, source_target_pairs={{0,96},{8,104},{1,97},{9,105},{2,98},{10,106},{3,99},{11,107},{32,... | collective-permute-start | bytes 147464 | tf_op jit(solution)/shard_map/ppermute | solution.py:46
  117.9 2.1 %collective-permute-start.30 = (bf16[64,384]{1,0:T(8,128)(2,1)}, bf16[64,384]{1,0:T(8,128)(2,1)S(1)}, u32[]{:S(2)}, u32[]{:S(2)}) collective-permute-start(bf16[64,384]{1,0:T(8,128)(2,1)} %get-tuple-element.60), channel_id=1, source_target_pairs={{0,72},{8,64},{1,73},{9,65},{2,74},{10,66},{3,75},{11,67},{32,104}... | collective-permute-start | bytes 147464 | tf_op jit(solution)/shard_map/ppermute | solution.py:46
  120.0 1.5 %collective-permute-start.31 = (bf16[64,384]{1,0:T(8,128)(2,1)}, bf16[64,384]{1,0:T(8,128)(2,1)S(1)}, u32[]{:S(2)}, u32[]{:S(2)}) collective-permute-start(bf16[64,384]{1,0:T(8,128)(2,1)} %get-tuple-element.61), channel_id=1, source_target_pairs={{0,32},{8,40},{1,33},{9,41},{2,34},{10,42},{3,35},{11,43},{32,64},... | collective-permute-start | bytes 147464 | tf_op jit(solution)/shard_map/ppermute | solution.py:46
  122.2 1.6 %collective-permute-done.30.refs_5_ = bf16[64,384]{1,0:T(8,128)(2,1)S(1)} collective-permute-done((bf16[64,384]{1,0:T(8,128)(2,1)}, bf16[64,384]{1,0:T(8,128)(2,1)S(1)}, u32[]{:S(2)}, u32[]{:S(2)}) %collective-permute-start.30) | collective-permute-done | bytes 49184 | tf_op jit(solution)/shard_map/ppermute | solution.py:46
  124.8 1.8 %collective-permute-done.32.refs_7_ = bf16[64,384]{1,0:T(8,128)(2,1)S(1)} collective-permute-done((bf16[64,384]{1,0:T(8,128)(2,1)}, bf16[64,384]{1,0:T(8,128)(2,1)S(1)}, u32[]{:S(2)}, u32[]{:S(2)}) %collective-permute-start.32) | collective-permute-done | bytes 49184 | tf_op jit(solution)/shard_map/ppermute | solution.py:46
  127.2 1.9 %shard_map.78 = bf16[64,3072]{1,0:T(8,128)(2,1)} custom-call(s32[8]{0:T(128)} %fusion.3.at_ref, s32[1]{0:T(128)S(6)} %copy.8.level_ref, f32[16,3072]{1,0:T(8,128)} %gates_ref.1, bf16[64,384]{1,0:T(8,128)(2,1)} %get-tuple-element.55.refs_0_, bf16[64,384]{1,0:T(8,128)(2,1)} %copy-done.25, bf16[64,384]{1,0:T(8,128)(2,1)} %copy-done.26, ...), custom_call_target="tpu_custom_call" | custom-call | tf_op jit(solution)/shard_map/pallas_call | solution.py:339
  (133 shorter events, 19.1 us)
Async XLA Ops:
  4.2 8.4 %collective-permute-start = (bf16[208,384]{1,0:T(8,128)(2,1)}, bf16[208,384]{1,0:T(8,128)(2,1)S(1)}, u32[]{:S(2)}, u32[]{:S(2)}) collective-permute-start(bf16[208,384]{1,0:T(8,128)(2,1)} %get-tuple-element.35), channel_id=1, source_target_pairs={{0,8},{8,0},{1,9},{9,1},{2,10},{10,2},{3,11},{11,3},{32,40},{40,32... | collective-permute-start | bytes 479240 | tf_op jit(solution)/shard_map/ppermute | solution.py:46
  5.6 8.4 %collective-permute-start.1 = (bf16[208,384]{1,0:T(8,128)(2,1)}, bf16[208,384]{1,0:T(8,128)(2,1)S(1)}, u32[]{:S(2)}, u32[]{:S(2)}) collective-permute-start(bf16[208,384]{1,0:T(8,128)(2,1)} %get-tuple-element.36), channel_id=1, source_target_pairs={{0,32},{8,40},{1,33},{9,41},{2,34},{10,42},{3,35},{11,43},{32,64},... | collective-permute-start | bytes 479240 | tf_op jit(solution)/shard_map/ppermute | solution.py:46
  7.0 9.4 %collective-permute-start.2 = (bf16[208,384]{1,0:T(8,128)(2,1)}, bf16[208,384]{1,0:T(8,128)(2,1)S(1)}, u32[]{:S(2)}, u32[]{:S(2)}) collective-permute-start(bf16[208,384]{1,0:T(8,128)(2,1)} %get-tuple-element.37), channel_id=1, source_target_pairs={{0,40},{8,32},{1,41},{9,33},{2,42},{10,34},{3,43},{11,35},{32,72},... | collective-permute-start | bytes 479240 | tf_op jit(solution)/shard_map/ppermute | solution.py:46
  8.5 12.3 %collective-permute-start.3 = (bf16[208,384]{1,0:T(8,128)(2,1)}, bf16[208,384]{1,0:T(8,128)(2,1)S(1)}, u32[]{:S(2)}, u32[]{:S(2)}) collective-permute-start(bf16[208,384]{1,0:T(8,128)(2,1)} %get-tuple-element.38), channel_id=1, source_target_pairs={{0,64},{8,72},{1,65},{9,73},{2,66},{10,74},{3,67},{11,75},{32,96},... | collective-permute-start | bytes 479240 | tf_op jit(solution)/shard_map/ppermute | solution.py:46
  9.6 14.8 %collective-permute-start.4 = (bf16[208,384]{1,0:T(8,128)(2,1)}, bf16[208,384]{1,0:T(8,128)(2,1)S(1)}, u32[]{:S(2)}, u32[]{:S(2)}) collective-permute-start(bf16[208,384]{1,0:T(8,128)(2,1)} %get-tuple-element.39), channel_id=1, source_target_pairs={{0,72},{8,64},{1,73},{9,65},{2,74},{10,66},{3,75},{11,67},{32,104}... | collective-permute-start | bytes 479240 | tf_op jit(solution)/shard_map/ppermute | solution.py:46
  12.6 11.9 %collective-permute-start.5 = (bf16[208,384]{1,0:T(8,128)(2,1)}, bf16[208,384]{1,0:T(8,128)(2,1)S(1)}, u32[]{:S(2)}, u32[]{:S(2)}) collective-permute-start(bf16[208,384]{1,0:T(8,128)(2,1)} %get-tuple-element.40), channel_id=1, source_target_pairs={{0,96},{8,104},{1,97},{9,105},{2,98},{10,106},{3,99},{11,107},{32,... | collective-permute-start | bytes 479240 | tf_op jit(solution)/shard_map/ppermute | solution.py:46
  14.0 11.3 %collective-permute-start.6 = (bf16[208,384]{1,0:T(8,128)(2,1)}, bf16[208,384]{1,0:T(8,128)(2,1)S(1)}, u32[]{:S(2)}, u32[]{:S(2)}) collective-permute-start(bf16[208,384]{1,0:T(8,128)(2,1)} %get-tuple-element.41), channel_id=1, source_target_pairs={{0,104},{8,96},{1,105},{9,97},{2,106},{10,98},{3,107},{11,99},{32,... | collective-permute-start | bytes 479240 | tf_op jit(solution)/shard_map/ppermute | solution.py:46
  28.6 9.2 %collective-permute-start.7 = (f32[8,128]{1,0:T(8,128)}, f32[8,128]{1,0:T(8,128)S(1)}, u32[]{:S(2)}, u32[]{:S(2)}) collective-permute-start(f32[8,128]{1,0:T(8,128)} %get-tuple-element.42), channel_id=1, source_target_pairs={{0,16},{8,24},{1,17},{9,25},{2,18},{10,26},{3,19},{11,27},{32,48},... | collective-permute-start | bytes 12296 | tf_op jit(solution)/shard_map/ppermute | solution.py:46
  31.3 7.2 %collective-permute-start.8 = (bf16[512,128]{1,0:T(8,128)(2,1)}, bf16[512,128]{1,0:T(8,128)(2,1)S(1)}, u32[]{:S(2)}, u32[]{:S(2)}) collective-permute-start(bf16[512,128]{1,0:T(8,128)(2,1)} %get-tuple-element.43), channel_id=1, source_target_pairs={{0,4},{8,9},{1,5},{9,10},{2,6},{10,11},{3,7},{11,8},{32,36},{40,41... | collective-permute-start | bytes 393224 | tf_op jit(solution)/shard_map/ppermute | solution.py:46
  33.0 7.3 %collective-permute-start.9 = (bf16[512,128]{1,0:T(8,128)(2,1)}, bf16[512,128]{1,0:T(8,128)(2,1)S(1)}, u32[]{:S(2)}, u32[]{:S(2)}) collective-permute-start(bf16[512,128]{1,0:T(8,128)(2,1)} %get-tuple-element.43), channel_id=1, source_target_pairs={{0,16},{8,10},{1,17},{9,11},{2,18},{10,8},{3,19},{11,9},{32,48},{4... | collective-permute-start | bytes 393224 | tf_op jit(solution)/shard_map/ppermute | solution.py:46
  36.3 5.2 %collective-permute-start.10 = (bf16[512,128]{1,0:T(8,128)(2,1)}, bf16[512,128]{1,0:T(8,128)(2,1)S(1)}, u32[]{:S(2)}, u32[]{:S(2)}) collective-permute-start(bf16[512,128]{1,0:T(8,128)(2,1)} %get-tuple-element.43), channel_id=1, source_target_pairs={{0,20},{8,11},{1,21},{9,8},{2,22},{10,9},{3,23},{11,10},{32,52},{4... | collective-permute-start | bytes 393224 | tf_op jit(solution)/shard_map/ppermute | solution.py:46
  37.0 9.2 %collective-permute-start.17 = (bf16[1024,128]{1,0:T(8,128)(2,1)}, bf16[1024,128]{1,0:T(8,128)(2,1)S(1)}, u32[]{:S(2)}, u32[]{:S(2)}) collective-permute-start(bf16[1024,128]{1,0:T(8,128)(2,1)} %get-tuple-element.49), channel_id=1, source_target_pairs={{0,4},{8,9},{1,5},{9,10},{2,6},{10,11},{3,7},{11,8},{32,36},{40,41... | collective-permute-start | bytes 786440 | tf_op jit(solution)/shard_map/ppermute | solution.py:46
  37.7 10.3 %collective-permute-start.11 = (bf16[1024,128]{1,0:T(8,128)(2,1)}, bf16[1024,128]{1,0:T(8,128)(2,1)S(1)}, u32[]{:S(2)}, u32[]{:S(2)}) collective-permute-start(bf16[1024,128]{1,0:T(8,128)(2,1)} %get-tuple-element.44), channel_id=1, source_target_pairs={{0,1},{8,12},{1,2},{9,13},{2,3},{10,14},{3,0},{11,15},{32,33},{40,... | collective-permute-start | bytes 786440 | tf_op jit(solution)/shard_map/ppermute | solution.py:46
  38.5 9.7 %collective-permute-start.12 = (bf16[1024,128]{1,0:T(8,128)(2,1)}, bf16[1024,128]{1,0:T(8,128)(2,1)S(1)}, u32[]{:S(2)}, u32[]{:S(2)}) collective-permute-start(bf16[1024,128]{1,0:T(8,128)(2,1)} %get-tuple-element.44), channel_id=1, source_target_pairs={{0,2},{8,24},{1,3},{9,25},{2,0},{10,26},{3,1},{11,27},{32,34},{40,... | collective-permute-start | bytes 786440 | tf_op jit(solution)/shard_map/ppermute | solution.py:46
  40.2 10.2 %collective-permute-start.13 = (bf16[1024,128]{1,0:T(8,128)(2,1)}, bf16[1024,128]{1,0:T(8,128)(2,1)S(1)}, u32[]{:S(2)}, u32[]{:S(2)}) collective-permute-start(bf16[1024,128]{1,0:T(8,128)(2,1)} %get-tuple-element.44), channel_id=1, source_target_pairs={{0,3},{8,28},{1,0},{9,29},{2,1},{10,30},{3,2},{11,31},{32,35},{40,... | collective-permute-start | bytes 786440 | tf_op jit(solution)/shard_map/ppermute | solution.py:46
  41.4 25.0 %collective-permute-start.20 = (bf16[2048,128]{1,0:T(8,128)(2,1)}, bf16[2048,128]{1,0:T(8,128)(2,1)S(1)}, u32[]{:S(2)}, u32[]{:S(2)}) collective-permute-start(bf16[2048,128]{1,0:T(8,128)(2,1)} %get-tuple-element.50), channel_id=1, source_target_pairs={{0,1},{8,12},{1,2},{9,13},{2,3},{10,14},{3,0},{11,15},{32,33},{40,... | collective-permute-start | bytes 1572872 | tf_op jit(solution)/shard_map/ppermute | solution.py:46
  46.2 20.3 %collective-permute-start.21 = (bf16[2048,128]{1,0:T(8,128)(2,1)}, bf16[2048,128]{1,0:T(8,128)(2,1)S(1)}, u32[]{:S(2)}, u32[]{:S(2)}) collective-permute-start(bf16[2048,128]{1,0:T(8,128)(2,1)} %get-tuple-element.50), channel_id=1, source_target_pairs={{0,2},{8,24},{1,3},{9,25},{2,0},{10,26},{3,1},{11,27},{32,34},{40,... | collective-permute-start | bytes 1572872 | tf_op jit(solution)/shard_map/ppermute | solution.py:46
  48.0 18.5 %collective-permute-start.22 = (bf16[2048,128]{1,0:T(8,128)(2,1)}, bf16[2048,128]{1,0:T(8,128)(2,1)S(1)}, u32[]{:S(2)}, u32[]{:S(2)}) collective-permute-start(bf16[2048,128]{1,0:T(8,128)(2,1)} %get-tuple-element.50), channel_id=1, source_target_pairs={{0,3},{8,28},{1,0},{9,29},{2,1},{10,30},{3,2},{11,31},{32,35},{40,... | collective-permute-start | bytes 1572872 | tf_op jit(solution)/shard_map/ppermute | solution.py:46
  48.2 18.1 %collective-permute-start.18 = (bf16[1024,128]{1,0:T(8,128)(2,1)}, bf16[1024,128]{1,0:T(8,128)(2,1)S(1)}, u32[]{:S(2)}, u32[]{:S(2)}) collective-permute-start(bf16[1024,128]{1,0:T(8,128)(2,1)} %get-tuple-element.49), channel_id=1, source_target_pairs={{0,16},{8,10},{1,17},{9,11},{2,18},{10,8},{3,19},{11,9},{32,48},{4... | collective-permute-start | bytes 786440 | tf_op jit(solution)/shard_map/ppermute | solution.py:46
  50.4 16.0 %collective-permute-start.19 = (bf16[1024,128]{1,0:T(8,128)(2,1)}, bf16[1024,128]{1,0:T(8,128)(2,1)S(1)}, u32[]{:S(2)}, u32[]{:S(2)}) collective-permute-start(bf16[1024,128]{1,0:T(8,128)(2,1)} %get-tuple-element.49), channel_id=1, source_target_pairs={{0,20},{8,11},{1,21},{9,8},{2,22},{10,9},{3,23},{11,10},{32,52},{4... | collective-permute-start | bytes 786440 | tf_op jit(solution)/shard_map/ppermute | solution.py:46
  66.4 27.9 %collective-permute-start.14 = (bf16[544,128]{1,0:T(8,128)(2,1)}, bf16[544,128]{1,0:T(8,128)(2,1)S(1)}, u32[]{:S(2)}, u32[]{:S(2)}) collective-permute-start(bf16[544,128]{1,0:T(8,128)(2,1)} %get-tuple-element.46), channel_id=1, source_target_pairs={{0,20},{8,11},{1,21},{9,8},{2,22},{10,9},{3,23},{11,10},{32,52},{4... | collective-permute-start | bytes 417800 | tf_op jit(solution)/shard_map/ppermute | solution.py:46
  88.7 16.0 %collective-permute-start.23 = (bf16[1088,128]{1,0:T(8,128)(2,1)}, bf16[1088,128]{1,0:T(8,128)(2,1)S(1)}, u32[]{:S(2)}, u32[]{:S(2)}) collective-permute-start(bf16[1088,128]{1,0:T(8,128)(2,1)} %get-tuple-element.52), channel_id=1, source_target_pairs={{0,20},{8,11},{1,21},{9,8},{2,22},{10,9},{3,23},{11,10},{32,52},{4... | collective-permute-start | bytes 835592 | tf_op jit(solution)/shard_map/ppermute | solution.py:46
  91.3 13.4 %collective-permute-start.24 = (bf16[1088,128]{1,0:T(8,128)(2,1)}, bf16[1088,128]{1,0:T(8,128)(2,1)S(1)}, u32[]{:S(2)}, u32[]{:S(2)}) collective-permute-start(bf16[1088,128]{1,0:T(8,128)(2,1)} %get-tuple-element.53), channel_id=1, source_target_pairs={{0,16},{8,10},{1,17},{9,11},{2,18},{10,8},{3,19},{11,9},{32,48},{4... | collective-permute-start | bytes 835592 | tf_op jit(solution)/shard_map/ppermute | solution.py:46
  92.0 12.7 %collective-permute-start.25 = (bf16[1088,128]{1,0:T(8,128)(2,1)}, bf16[1088,128]{1,0:T(8,128)(2,1)S(1)}, u32[]{:S(2)}, u32[]{:S(2)}) collective-permute-start(bf16[1088,128]{1,0:T(8,128)(2,1)} %get-tuple-element.54), channel_id=1, source_target_pairs={{0,4},{8,9},{1,5},{9,10},{2,6},{10,11},{3,7},{11,8},{32,36},{40,41... | collective-permute-start | bytes 835592 | tf_op jit(solution)/shard_map/ppermute | solution.py:46
  92.0 11.1 %collective-permute-start.15 = (bf16[544,128]{1,0:T(8,128)(2,1)S(1)}, bf16[544,128]{1,0:T(8,128)(2,1)S(1)}, u32[]{:S(2)}, u32[]{:S(2)}) collective-permute-start(bf16[544,128]{1,0:T(8,128)(2,1)S(1)} %copy-done.36), channel_id=1, source_target_pairs={{0,16},{8,10},{1,17},{9,11},{2,18},{10,8},{3,19},{11,9},{32,48},{4... | collective-permute-start | bytes 417800 | tf_op jit(solution)/shard_map/ppermute | solution.py:46
  94.3 10.4 %collective-permute-start.16 = (bf16[544,128]{1,0:T(8,128)(2,1)S(1)}, bf16[544,128]{1,0:T(8,128)(2,1)S(1)}, u32[]{:S(2)}, u32[]{:S(2)}) collective-permute-start(bf16[544,128]{1,0:T(8,128)(2,1)S(1)} %copy-done.35), channel_id=1, source_target_pairs={{0,4},{8,9},{1,5},{9,10},{2,6},{10,11},{3,7},{11,8},{32,36},{40,41... | collective-permute-start | bytes 417800 | tf_op jit(solution)/shard_map/ppermute | solution.py:46
  108.6 11.3 %collective-permute-start.26 = (bf16[64,384]{1,0:T(8,128)(2,1)}, bf16[64,384]{1,0:T(8,128)(2,1)S(1)}, u32[]{:S(2)}, u32[]{:S(2)}) collective-permute-start(bf16[64,384]{1,0:T(8,128)(2,1)} %get-tuple-element.56), channel_id=1, source_target_pairs={{0,8},{8,0},{1,9},{9,1},{2,10},{10,2},{3,11},{11,3},{32,40},{40,32... | collective-permute-start | bytes 147464 | tf_op jit(solution)/shard_map/ppermute | solution.py:46
  113.4 8.1 %collective-permute-start.27 = (bf16[64,384]{1,0:T(8,128)(2,1)}, bf16[64,384]{1,0:T(8,128)(2,1)S(1)}, u32[]{:S(2)}, u32[]{:S(2)}) collective-permute-start(bf16[64,384]{1,0:T(8,128)(2,1)} %get-tuple-element.57), channel_id=1, source_target_pairs={{0,96},{8,104},{1,97},{9,105},{2,98},{10,106},{3,99},{11,107},{32,... | collective-permute-start | bytes 147464 | tf_op jit(solution)/shard_map/ppermute | solution.py:46
  116.5 5.7 %collective-permute-start.28 = (bf16[64,384]{1,0:T(8,128)(2,1)}, bf16[64,384]{1,0:T(8,128)(2,1)S(1)}, u32[]{:S(2)}, u32[]{:S(2)}) collective-permute-start(bf16[64,384]{1,0:T(8,128)(2,1)} %get-tuple-element.58), channel_id=1, source_target_pairs={{0,104},{8,96},{1,105},{9,97},{2,106},{10,98},{3,107},{11,99},{32,... | collective-permute-start | bytes 147464 | tf_op jit(solution)/shard_map/ppermute | solution.py:46
  116.5 5.6 %collective-permute-start.29 = (bf16[64,384]{1,0:T(8,128)(2,1)}, bf16[64,384]{1,0:T(8,128)(2,1)S(1)}, u32[]{:S(2)}, u32[]{:S(2)}) collective-permute-start(bf16[64,384]{1,0:T(8,128)(2,1)} %get-tuple-element.59), channel_id=1, source_target_pairs={{0,64},{8,72},{1,65},{9,73},{2,66},{10,74},{3,67},{11,75},{32,96},... | collective-permute-start | bytes 147464 | tf_op jit(solution)/shard_map/ppermute | solution.py:46
  117.9 5.9 %collective-permute-start.30 = (bf16[64,384]{1,0:T(8,128)(2,1)}, bf16[64,384]{1,0:T(8,128)(2,1)S(1)}, u32[]{:S(2)}, u32[]{:S(2)}) collective-permute-start(bf16[64,384]{1,0:T(8,128)(2,1)} %get-tuple-element.60), channel_id=1, source_target_pairs={{0,72},{8,64},{1,73},{9,65},{2,74},{10,66},{3,75},{11,67},{32,104}... | collective-permute-start | bytes 147464 | tf_op jit(solution)/shard_map/ppermute | solution.py:46
  121.5 5.1 %collective-permute-start.32 = (bf16[64,384]{1,0:T(8,128)(2,1)}, bf16[64,384]{1,0:T(8,128)(2,1)S(1)}, u32[]{:S(2)}, u32[]{:S(2)}) collective-permute-start(bf16[64,384]{1,0:T(8,128)(2,1)} %get-tuple-element.62), channel_id=1, source_target_pairs={{0,40},{8,32},{1,41},{9,33},{2,42},{10,34},{3,43},{11,35},{32,72},... | collective-permute-start | bytes 147464 | tf_op jit(solution)/shard_map/ppermute | solution.py:46
  (39 other events, 223.0 us)
where the time goes:
time: 129 us
  starting transfers between devices  46.7 us (36%)
  Pallas kernels  42.9 us (33%)
  waiting for transfers between devices  29.2 us (23%)
  local copies, waits for them, and re-layouts  5.74 us (4%)
  other arithmetic  2.92 us (2%)
  between operations  1.67 us (1%)
    ppermute x33, starting transfers between devices, moved(): return lax.ppermute(array, BOTH, pairs)  46.7 us
    pallas_call x2, Pallas kernels, attend(): call(functools.partial(attend_kernel, count), [shape(count * (SET + META)...  33 us
    ppermute x33, waiting for transfers between devices, moved(): return lax.ppermute(array, BOTH, pairs)  29.2 us
    unnamed x76, local copies, waits for them, and re-layouts  5.05 us
    pallas_call x1, Pallas kernels, local(): call(combine_kernel, [shape(ROWS, WIDTH)] * GROUP, [SMEM] + [VMEM] * len(...  2.99 us
  transfers between devices with their start and end apart: 33, of which 12 were waited for; matrix products, arithmetic and copies ran while one was open for 2% of the time, Pallas kernels for 26%

commit v1 on v0

--- a/solution.py
+++ b/solution.py
@@ -28,6 +28,7 @@
 BOTH = ("span", "tok")
 VMEM = pl.BlockSpec(memory_space=pltpu.VMEM)
 SMEM = pl.BlockSpec(memory_space=pltpu.SMEM)
+ANY = pl.BlockSpec(memory_space=pl.ANY)
 
 
 def device_at(x, y, z, core):
@@ -69,19 +70,50 @@
 
 
 def spread_kernel(*refs):
-    in_refs, out_refs = refs[:GROUP], refs[GROUP:]
-    for j in range(GROUP):
-        ref = in_refs[j]
-        for p, part in enumerate(PARTS):
-            q_ref, kv_ref = out_refs[2 * p], out_refs[2 * p + 1]
-            for i, h in enumerate(part):
-                columns = slice(h * HEAD_DIM, (h + 1) * HEAD_DIM)
-                q_ref[i * SET + j * ROWS : i * SET + (j + 1) * ROWS, :] = ref[0:ROWS, columns]
+    in_refs, out_refs, sems = refs[:GROUP], refs[GROUP:-1], refs[-1]
+    copies = []
+
+    def send(source, target):
+        copy = pltpu.make_async_copy(source, target, sems.at[len(copies)])
+        copy.start()
+        copies.append(copy)
+
+    for p, part in enumerate(PARTS):
+        q_ref, kv_ref = out_refs[2 * p], out_refs[2 * p + 1]
+        for i, h in enumerate(part):
+            columns = pl.ds(h * HEAD_DIM, HEAD_DIM)
+            for j, ref in enumerate(in_refs):
+                send(ref.at[pl.ds(0, ROWS), columns], q_ref.at[i, j])
                 for t in range(2):
-                    base = (2 * i + t) * SET + j * ROWS
-                    kv_ref[base : base + ROWS, :] = ref[(t + 1) * ROWS : (t + 2) * ROWS, columns]
-        row = ref[3 * ROWS : 3 * ROWS + 16, 0:HEAD_DIM].astype(jnp.float32)
-        out_refs[-1][j : j + 1, :] = row[0:1]
+                    send(ref.at[pl.ds((t + 1) * ROWS, ROWS), columns], kv_ref.at[i, t, j])
+    for j, ref in enumerate(in_refs):
+        send(ref.at[pl.ds(3 * ROWS, 16), pl.ds(0, HEAD_DIM)], out_refs[-1].at[j])
+    for copy in copies:
+        copy.wait()
+
+
+def fetched(kernel, small, count, *refs):
+    sems, held = refs[-1], refs[-1 - count : -1]
+    copies = [
+        pltpu.make_async_copy(refs[small + n], held[n], sems.at[n]) for n in range(count)
+    ]
+    for copy in copies:
+        copy.start()
+    for copy in copies:
+        copy.wait()
+    kernel(*refs[:small], *held, *refs[small + count : -1 - count])
+
+
+def call_fetched(kernel, shapes, specs, ready, pieces):
+    count = len(pieces)
+    return pl.pallas_call(
+        functools.partial(fetched, kernel, len(ready), count),
+        out_shape=shapes,
+        in_specs=specs + [ANY] * count,
+        out_specs=jax.tree.map(lambda unused: VMEM, shapes),
+        scratch_shapes=[pltpu.VMEM(piece.shape, piece.dtype) for piece in pieces]
+        + [pltpu.SemaphoreType.DMA((count,))],
+    )(*ready, *pieces)
 
 
 def together_in(count):
@@ -123,32 +155,38 @@
             rows = slice(i * TILE, (i + 1) * TILE)
             v_turned[h, :, rows] = rows_of(v_all, h, i).T
 
+    chains = [(t, h) for t in range(together) for h in range(count)]
+
+    def trips_of(first):
+        seen = [table_ref[limits + first * together + t] for t in range(together)]
+        return jnp.maximum((functools.reduce(jnp.maximum, seen) + STEP - 1) // STEP, 1)
+
+    def fill(first, g):
+        for c, (t, h) in enumerate(chains):
+            pick = first * together + t
+            at = pick * TILES + g * STEP
+            rows = [rows_of(k_all, h, table_ref[at + u]) for u in range(STEP)]
+            score_ref[c] = lax.dot_general(
+                jnp.concatenate(rows, axis=0),
+                rows_of(q_all, h, pick),
+                (((1,), (1,)), ((), ())),
+                preferred_element_type=jnp.float32,
+            )
+
     def tiles(first, unused):
         picks = [first * together + t for t in range(together)]
         seen = [table_ref[limits + i] for i in picks]
-        trips = functools.reduce(jnp.maximum, seen)
-        chains = [(t, h) for t in range(together) for h in range(count)]
+        trips = trips_of(first)
         starts = [pl.multiple_of(i * TILE, TILE) for i in picks]
-
-        def fill(g):
-            for c, (t, h) in enumerate(chains):
-                rows = [rows_of(k_all, h, place(t, g, u)) for u in range(STEP)]
-                score_ref[c] = lax.dot_general(
-                    jnp.concatenate(rows, axis=0),
-                    rows_of(q_all, h, picks[t]),
-                    (((1,), (1,)), ((), ())),
-                    preferred_element_type=jnp.float32,
-                )
 
         def place(t, g, u):
             return table_ref[picks[t] * TILES + g * STEP + u]
-
-        fill(0)
 
         def step(g, carry):
             parts = [range(at, at + SUB) for at in range(0, STEP, SUB)]
             scores = [score_ref[c] for c in range(len(chains))]
-            fill(jnp.minimum(g + 1, TILES // STEP - 1))
+            last = (g + 1 >= trips).astype(jnp.int32)
+            fill(jnp.minimum(first + last, TILES // together - 1), (1 - last) * (g + 1))
             result = list(carry)
             for part in parts:
                 for c, (t, h) in enumerate(chains):
@@ -165,7 +203,8 @@
                     added = functools.reduce(jnp.add, weights).reshape(TILE // 8, 8, TILE)
                     total = total * shrink + jnp.sum(added, axis=0)
                     weight = jnp.concatenate([w.astype(jnp.bfloat16) for w in weights], axis=0)
-                    columns = [v_turned[h, :, pl.ds(pl.multiple_of(place(t, g, u) * TILE, TILE), TILE)] for u in part]
+                    ats = [pl.multiple_of(place(t, g, u) * TILE, TILE) for u in part]
+                    columns = [v_turned[h, :, pl.ds(at, TILE)] for at in ats]
                     acc = acc * shrink + jnp.dot(
                         jnp.concatenate(columns, axis=1),
                         weight,
@@ -179,7 +218,7 @@
             jnp.zeros((8, TILE), jnp.float32),
             jnp.zeros((HEAD_DIM, TILE), jnp.float32),
         )
-        final = lax.fori_loop(0, (trips + STEP - 1) // STEP, step, [empty] * len(chains))
+        final = lax.fori_loop(0, trips, step, [empty] * len(chains))
         for (t, h), (top, total, acc) in zip(chains, final):
             total = jnp.sum(total, axis=0, keepdims=True)
             total = jnp.where(total > 0.0, total, 1.0)
@@ -187,6 +226,7 @@
             lse_ref[h, picks[t] % 2, pl.ds(picks[t] // 2, 1), :] = top * factor + jnp.log2(total)
         return unused
 
+    fill(0, 0)
     lax.fori_loop(0, TILES // together, tiles, 0)
     for h in range(count):
         for d in range(RING):
@@ -206,13 +246,11 @@
 
 
 def attend(count, table, q, kv):
-    q = [piece.reshape(count, GROUP, ROWS, HEAD_DIM) for piece in q]
-    kv = [piece.reshape(count, 2, GROUP, ROWS, HEAD_DIM) for piece in kv]
     pieces = pltpu.VMEM((count, GROUP, RING, ROWS, HEAD_DIM), jnp.bfloat16)
     return call(
         functools.partial(attend_kernel, count),
         [shape(count * (SET + META), HEAD_DIM)] * RING,
-        [SMEM] + [pl.BlockSpec(memory_space=pl.ANY)] * (2 * RING),
+        [SMEM] + [ANY] * (2 * RING),
         [pieces] * 3
         + [
             pltpu.VMEM((count, RING * SET, HEAD_DIM), jnp.bfloat16),
@@ -296,16 +334,24 @@
 
     shapes = []
     for part in PARTS:
-        shapes += [shape(len(part) * SET, HEAD_DIM), shape(len(part) * 2 * SET, HEAD_DIM)]
-    spread = call(
-        spread_kernel, shapes + [shape(GROUP, HEAD_DIM, jnp.float32)], [VMEM] * GROUP
+        shapes.append((len(part), GROUP, ROWS, HEAD_DIM))
+        shapes.append((len(part), 2, GROUP, ROWS, HEAD_DIM))
+    shapes = [jax.ShapeDtypeStruct(dims, jnp.bfloat16) for dims in shapes + [(GROUP, 16, HEAD_DIM)]]
+    spread = pl.pallas_call(
+        spread_kernel,
+        out_shape=shapes,
+        in_specs=[ANY] * GROUP,
+        out_specs=[ANY] * len(shapes),
+        scratch_shapes=[pltpu.SemaphoreType.DMA((3 * HEADS_DEV * GROUP + GROUP,))],
     )(*shared)
 
     tile = jnp.arange(TILES, dtype=jnp.int32)
     base = (y - tile // 4) % 4 * 4 + (core ^ tile // 2 % 2)
     wide_slots, near_slots = base + 2 * (tile % 2), base + 2 * half
-    near_mask = jnp.repeat(spread[-1], 2, axis=0)
-    far_mask = jnp.repeat(moved(spread[-1], dx=2), 2, axis=0)
+    near_mask, far_mask = [
+        jnp.repeat(rows[:, 0, :SPANS].astype(jnp.float32), 2, axis=0)
+        for rows in (spread[-1], moved(spread[-1], dx=2))
+    ]
     wide_mask = jnp.where((tile % 2 == half)[:, None], near_mask, far_mask)
     first = core == 0
     ring = jnp.arange(RING, dtype=jnp.int32)
@@ -332,12 +378,14 @@
         for d in range(1, RING):
             pieces.append(moved(parts[d], dx=-d, swap=1))
 
-    mixed = call(
-        combine_kernel, [shape(ROWS, WIDTH)] * GROUP, [SMEM] + [VMEM] * len(pieces)
-    )(table, *pieces)
+    mixed = call_fetched(combine_kernel, [shape(ROWS, WIDTH)] * GROUP, [SMEM], [table], pieces)
     returned = [mixed[0]] + [moved(mixed[j], **backs[j]) for j in range(1, GROUP)]
-    result = call(finish_kernel, shape(ROWS, GROUP * WIDTH), [SMEM, SMEM] + [VMEM] * (GROUP + 1))(
-        target, levels, gates, *returned
+    result = call_fetched(
+        finish_kernel,
+        shape(ROWS, GROUP * WIDTH),
+        [SMEM, SMEM, VMEM],
+        [target, levels, gates],
+        returned,
     )
     return result[None]
 

time: 129 us -> 166 us (1.29)
  Pallas kernels: 42.9 us -> 75.8 us
  waiting for transfers between devices: 29.2 us -> 32.9 us
    pallas_call x3, Pallas kernels: 7.47 us -> 45.2 us  [the longest x1 38.5 us: local(): pl.pallas_call(spread_kernel, out_shape=shapes, in_specs=[ANY] * GROUP, o...]
    pallas_call x2, Pallas kernels: 33 us -> 28.2 us  [attend(): call(functools.partial(attend_kernel, count), [shape(count * (SET + META)...]
    ppermute x33, waiting for transfers between devices: 29.2 us -> 32.9 us  [moved(): return lax.ppermute(array, BOTH, pairs)]
    unnamed x76 -> x74, local copies, waits for them, and re-layouts: 5.05 us -> 4.32 us
  transfers between devices with their start and end apart: 33 -> 33, of which waited for: 12 -> 12; matrix products, arithmetic and copies ran while one was open for 2% -> 2% of each run, Pallas kernels for 26% -> 17%
where the time goes in v1:
time: 166 us; the launch traced here: 165 us
  Pallas kernels  75.8 us (46%)
  starting transfers between devices  46.2 us (28%)
  waiting for transfers between devices  32.9 us (20%)
  local copies, waits for them, and re-layouts  5.01 us (3%)
  other arithmetic  3.7 us (2%)
  between operations  1.9 us (1%)
    ppermute x33, starting transfers between devices, moved(): return lax.ppermute(array, BOTH, pairs)  46.2 us
    pallas_call x1, Pallas kernels, local(): pl.pallas_call(spread_kernel, out_shape=shapes, in_specs=[ANY] * GROUP, o...  38.5 us
    ppermute x33, waiting for transfers between devices, moved(): return lax.ppermute(array, BOTH, pairs)  32.9 us
    pallas_call x2, Pallas kernels, attend(): call(functools.partial(attend_kernel, count), [shape(count * (SET + META)...  28.2 us
    pallas_call x2, Pallas kernels, call_fetched(): pl.pallas_call(functools.partial(fetched, kernel, len(ready), count), out...  6.62 us
    unnamed x74, local copies, waits for them, and re-layouts  4.32 us
  transfers between devices with their start and end apart: 33, of which 12 were waited for; matrix products, arithmetic and copies ran while one was open for 2% of the time, Pallas kernels for 17%

profile of v1, /device:TPU:1, one launch (start us, length us, event | category | flops | bytes accessed | tf_op | source)
XLA Modules:
  0.0 165.4 jit_solution(17751739370047440536)
XLA Ops:
  1.8 2.4 %shard_map.73 = (bf16[208,384]{1,0:T(8,128)(2,1)}, bf16[208,384]{1,0:T(8,128)(2,1)}, bf16[208,384]{1,0:T(8,128)(2,1)}, bf16[208,384]{1,0:T(8,128)(2,1)}, bf16[20...) custom-call(s32[8]{0:T(128)} %fusion.3.at_ref.refs_0_, ...), custom_call_target="tpu_custom_call" | custom-call | tf_op jit(solution)/shard_map/pallas_call | solution.py:328
  4.2 1.4 collective-permute-start
  5.6 1.4 collective-permute-start.1
  7.0 1.5 collective-permute-start.2
  9.6 2.2 %collective-permute-start.4 = (bf16[208,384]{1,0:T(8,128)(2,1)}, bf16[208,384]{1,0:T(8,128)(2,1)S(1)}, u32[]{:S(2)}, u32[]{:S(2)}) collective-permute-start(bf16[208,384]{1,0:T(8,128)(2,1)} %get-tuple-element.39), channel_id=1, source_target_pairs={{0,72},{8,64},{1,73},{9,65},{2,74},{10,66},{3,75},{11,67},{32,104}... | collective-permute-start | bytes 479240 | tf_op jit(solution)/shard_map/ppermute | solution.py:47
  13.1 1.4 collective-permute-start.5
  16.4 4.4 %collective-permute-done.3.refs_4_ = bf16[208,384]{1,0:T(8,128)(2,1)S(1)} collective-permute-done((bf16[208,384]{1,0:T(8,128)(2,1)}, bf16[208,384]{1,0:T(8,128)(2,1)S(1)}, u32[]{:S(2)}, u32[]{:S(2)}) %collective-permute-start.3) | collective-permute-done | bytes 159776 | tf_op jit(solution)/shard_map/ppermute | solution.py:47
  20.8 3.6 %collective-permute-done.4.refs_5_ = bf16[208,384]{1,0:T(8,128)(2,1)S(1)} collective-permute-done((bf16[208,384]{1,0:T(8,128)(2,1)}, bf16[208,384]{1,0:T(8,128)(2,1)S(1)}, u32[]{:S(2)}, u32[]{:S(2)}) %collective-permute-start.4) | collective-permute-done | bytes 159776 | tf_op jit(solution)/shard_map/ppermute | solution.py:47
  26.0 38.5 %shard_map.74 = (bf16[1,8,64,128]{3,2,1,0:T(8,128)(2,1)}, bf16[1,2,8,64,128]{4,3,2,1,0:T(8,128)(2,1)}, bf16[2,8,64,128]{3,2,1,0:T(8,128)(2,1)}, bf16[2,2,8,64,128]{4,3,2,1,0:T(8,128)(2,1)}, bf16[8,16,128]{2,1,0:T(8,128)(2,1)}) custom-call(bf16[208,384]{1,0:T(8,128)(2,1)} %get-tuple-element.34.refs_0_, bf16[208,384]{1,0:T(8,128)(2,1)} %copy-done.12, ...), custom_call_target="tpu_custom_call" | custom-call | tf_op jit(solution)/shard_map/pallas_call | solution.py:340
  64.6 2.8 %collective-permute-start.7 = (bf16[8,16,128]{2,1,0:T(8,128)(2,1)}, bf16[8,16,128]{2,1,0:T(8,128)(2,1)S(1)}, u32[]{:S(2)}, u32[]{:S(2)}) collective-permute-start(bf16[8,16,128]{2,1,0:T(8,128)(2,1)} %get-tuple-element.42), channel_id=1, source_target_pairs={{0,16},{8,24},{1,17},{9,25},{2,18},{10,26},{3,19},{11,27},{32,48},... | collective-permute-start | bytes 98312 | tf_op jit(solution)/shard_map/ppermute | solution.py:47
  68.1 3.8 %collective-permute-start.10 = (bf16[1,8,64,128]{3,2,1,0:T(8,128)(2,1)}, bf16[1,8,64,128]{3,2,1,0:T(8,128)(2,1)S(1)}, u32[]{:S(2)}, u32[]{:S(2)}) collective-permute-start(bf16[1,8,64,128]{3,2,1,0:T(8,128)(2,1)} %get-tuple-element.43.refs_0_), channel_id=1, source_target_pairs={{0,20},{8,11},{1,21},{9,8},{2,22},{10,9},{3,23},{11,10},{32,52},{4... | collective-permute-start | bytes 393224 | tf_op jit(solution)/shard_map/ppermute | solution.py:47
  71.9 1.3 collective-permute-start.9
  73.2 1.9 %collective-permute-start.17 = (bf16[2,8,64,128]{3,2,1,0:T(8,128)(2,1)}, bf16[2,8,64,128]{3,2,1,0:T(8,128)(2,1)S(1)}, u32[]{:S(2)}, u32[]{:S(2)}) collective-permute-start(bf16[2,8,64,128]{3,2,1,0:T(8,128)(2,1)} %get-tuple-element.49.refs_0_), channel_id=1, source_target_pairs={{0,4},{8,9},{1,5},{9,10},{2,6},{10,11},{3,7},{11,8},{32,36},{40,41... | collective-permute-start | bytes 786440 | tf_op jit(solution)/shard_map/ppermute | solution.py:47
  75.6 1.8 %collective-permute-start.12 = (bf16[1,2,8,64,128]{4,3,2,1,0:T(8,128)(2,1)}, bf16[1,2,8,64,128]{4,3,2,1,0:T(8,128)(2,1)S(1)}, u32[]{:S(2)}, u32[]{:S(2)}) collective-permute-start(bf16[1,2,8,64,128]{4,3,2,1,0:T(8,128)(2,1)} %get-tuple-element.44.refs_4_), channel_id=1, source_target_pairs={{0,2},{8,24},{1,3},{9,25},{2,0},{10,26},{3,1},{11,27},{32,34},{40,... | collective-permute-start | bytes 786440 | tf_op jit(solution)/shard_map/ppermute | solution.py:47
  77.4 1.4 collective-permute-done.8.refs_1_
  80.5 6.5 %collective-permute-done.17.refs_1_ = bf16[2,8,64,128]{3,2,1,0:T(8,128)(2,1)S(1)} collective-permute-done((bf16[2,8,64,128]{3,2,1,0:T(8,128)(2,1)}, bf16[2,8,64,128]{3,2,1,0:T(8,128)(2,1)S(1)}, u32[]{:S(2)}, u32[]{:S(2)}) %collective-permute-start.17) | collective-permute-done | bytes 262176 | tf_op jit(solution)/shard_map/ppermute | solution.py:47
  87.0 3.0 %collective-permute-start.22 = (bf16[2,2,8,64,128]{4,3,2,1,0:T(8,128)(2,1)}, bf16[2,2,8,64,128]{4,3,2,1,0:T(8,128)(2,1)S(1)}, u32[]{:S(2)}, u32[]{:S(2)}) collective-permute-start(bf16[2,2,8,64,128]{4,3,2,1,0:T(8,128)(2,1)} %get-tuple-element.50.refs_4_), channel_id=1, source_target_pairs={{0,3},{8,28},{1,0},{9,29},{2,1},{10,30},{3,2},{11,31},{32,35},{40,... | collective-permute-start | bytes 1572872 | tf_op jit(solution)/shard_map/ppermute | solution.py:47
  92.6 10.2 %shard_map.75 = (bf16[544,128]{1,0:T(8,128)(2,1)}, bf16[544,128]{1,0:T(8,128)(2,1)}, bf16[544,128]{1,0:T(8,128)(2,1)}, bf16[544,128]{1,0:T(8,128)(2,1)}) custom-call(s32[280]{0:T(512)} %pad_add_fusion.table_ref.refs_0_, bf16[1,8,64,128]{3,2,1,0:T(8,128)(2,1)} %get-tuple-element.43.refs_0_, bf16[1,8,64,128]{3,2,1,0:T(8,128)(2,1)} %copy-done.23, ...), custom_call_target="tpu_custom_call" | custom-call | tf_op jit(solution)/shard_map/pallas_call | solution.py:250
  102.8 3.2 %collective-permute-start.14 = (bf16[544,128]{1,0:T(8,128)(2,1)}, bf16[544,128]{1,0:T(8,128)(2,1)S(1)}, u32[]{:S(2)}, u32[]{:S(2)}) collective-permute-start(bf16[544,128]{1,0:T(8,128)(2,1)} %get-tuple-element.46), channel_id=1, source_target_pairs={{0,20},{8,11},{1,21},{9,8},{2,22},{10,9},{3,23},{11,10},{32,52},{4... | collective-permute-start | bytes 417800 | tf_op jit(solution)/shard_map/ppermute | solution.py:47
  108.1 18.0 %shard_map.76 = (bf16[1088,128]{1,0:T(8,128)(2,1)}, bf16[1088,128]{1,0:T(8,128)(2,1)}, bf16[1088,128]{1,0:T(8,128)(2,1)}, bf16[1088,128]{1,0:T(8,128)(2,1)}) custom-call(s32[280]{0:T(512)} %pad_add_fusion.table_ref.refs_0_, bf16[2,8,64,128]{3,2,1,0:T(8,128)(2,1)} %get-tuple-element.49.refs_0_, bf16[2,8,64,128]{3,2,1,0:T(8,128)(2,1)} %copy-done.9, ...), custom_call_target="tpu_custom_call" | custom-call | tf_op jit(solution)/shard_map/pallas_call | solution.py:250
  126.1 1.8 %collective-permute-start.23 = (bf16[1088,128]{1,0:T(8,128)(2,1)}, bf16[1088,128]{1,0:T(8,128)(2,1)S(1)}, u32[]{:S(2)}, u32[]{:S(2)}) collective-permute-start(bf16[1088,128]{1,0:T(8,128)(2,1)} %get-tuple-element.52), channel_id=1, source_target_pairs={{0,20},{8,11},{1,21},{9,8},{2,22},{10,9},{3,23},{11,10},{32,52},{4... | collective-permute-start | bytes 835592 | tf_op jit(solution)/shard_map/ppermute | solution.py:47
  128.6 2.6 %collective-permute-start.15 = (bf16[544,128]{1,0:T(8,128)(2,1)S(1)}, bf16[544,128]{1,0:T(8,128)(2,1)S(1)}, u32[]{:S(2)}, u32[]{:S(2)}) collective-permute-start(bf16[544,128]{1,0:T(8,128)(2,1)S(1)} %copy-done.35), channel_id=1, source_target_pairs={{0,16},{8,10},{1,17},{9,11},{2,18},{10,8},{3,19},{11,9},{32,48},{4... | collective-permute-start | bytes 417800 | tf_op jit(solution)/shard_map/ppermute | solution.py:47
  131.5 8.2 %collective-permute-done.15.refs_3_ = bf16[544,128]{1,0:T(8,128)(2,1)S(1)} collective-permute-done((bf16[544,128]{1,0:T(8,128)(2,1)S(1)}, bf16[544,128]{1,0:T(8,128)(2,1)S(1)}, u32[]{:S(2)}, u32[]{:S(2)}) %collective-permute-start.15) | collective-permute-done | bytes 139296 | tf_op jit(solution)/shard_map/ppermute | solution.py:47
  139.7 1.4 collective-permute-done.16.refs_4_
  142.0 3.8 %shard_map.77 = (bf16[64,384]{1,0:T(8,128)(2,1)}, bf16[64,384]{1,0:T(8,128)(2,1)}, bf16[64,384]{1,0:T(8,128)(2,1)}, bf16[64,384]{1,0:T(8,128)(2,1)}, bf16[64,384...) custom-call(s32[280]{0:T(512)} %pad_add_fusion.table_ref.refs_0_, ...), custom_call_target="tpu_custom_call" | custom-call | tf_op jit(solution)/shard_map/pallas_call | solution.py:109
  145.9 3.0 %collective-permute-start.26 = (bf16[64,384]{1,0:T(8,128)(2,1)}, bf16[64,384]{1,0:T(8,128)(2,1)S(1)}, u32[]{:S(2)}, u32[]{:S(2)}) collective-permute-start(bf16[64,384]{1,0:T(8,128)(2,1)} %get-tuple-element.56), channel_id=1, source_target_pairs={{0,8},{8,0},{1,9},{9,1},{2,10},{10,2},{3,11},{11,3},{32,40},{40,32... | collective-permute-start | bytes 147464 | tf_op jit(solution)/shard_map/ppermute | solution.py:47
  148.9 2.8 %collective-permute-start.27 = (bf16[64,384]{1,0:T(8,128)(2,1)}, bf16[64,384]{1,0:T(8,128)(2,1)S(1)}, u32[]{:S(2)}, u32[]{:S(2)}) collective-permute-start(bf16[64,384]{1,0:T(8,128)(2,1)} %get-tuple-element.57), channel_id=1, source_target_pairs={{0,96},{8,104},{1,97},{9,105},{2,98},{10,106},{3,99},{11,107},{32,... | collective-permute-start | bytes 147464 | tf_op jit(solution)/shard_map/ppermute | solution.py:47
  153.1 2.2 %collective-permute-start.30 = (bf16[64,384]{1,0:T(8,128)(2,1)}, bf16[64,384]{1,0:T(8,128)(2,1)S(1)}, u32[]{:S(2)}, u32[]{:S(2)}) collective-permute-start(bf16[64,384]{1,0:T(8,128)(2,1)} %get-tuple-element.60), channel_id=1, source_target_pairs={{0,72},{8,64},{1,73},{9,65},{2,74},{10,66},{3,75},{11,67},{32,104}... | collective-permute-start | bytes 147464 | tf_op jit(solution)/shard_map/ppermute | solution.py:47
  155.3 1.4 collective-permute-start.31
  157.5 1.6 collective-permute-done.30.refs_8_
  159.7 2.2 %collective-permute-done.32.refs_10_ = bf16[64,384]{1,0:T(8,128)(2,1)S(1)} collective-permute-done((bf16[64,384]{1,0:T(8,128)(2,1)}, bf16[64,384]{1,0:T(8,128)(2,1)S(1)}, u32[]{:S(2)}, u32[]{:S(2)}) %collective-permute-start.32) | collective-permute-done | bytes 49184 | tf_op jit(solution)/shard_map/ppermute | solution.py:47
  162.5 2.8 %shard_map.78 = bf16[64,3072]{1,0:T(8,128)(2,1)} custom-call(s32[8]{0:T(128)} %fusion.3.at_ref.refs_0_, s32[1]{0:T(128)S(6)} %copy.8.refs_1_, f32[16,3072]{1,0:T(8,128)} %refs_2_.1, bf16[64,384]{1,0:T(8,128)(2,1)} %get-tuple-element.55.refs_3_, bf16[64,384]{1,0:T(8,128)(2,1)} %copy-done.25, bf16[64,384]{1,0:T(8,128)(2,1)} %copy-done.26, ...), custom_call_target="tpu_custom_call" | custom-call | tf_op jit(solution)/shard_map/pallas_call | solution.py:109
  (133 shorter events, 18.9 us)
Async XLA Ops:
  4.2 8.9 %collective-permute-start = (bf16[208,384]{1,0:T(8,128)(2,1)}, bf16[208,384]{1,0:T(8,128)(2,1)S(1)}, u32[]{:S(2)}, u32[]{:S(2)}) collective-permute-start(bf16[208,384]{1,0:T(8,128)(2,1)} %get-tuple-element.35), channel_id=1, source_target_pairs={{0,8},{8,0},{1,9},{9,1},{2,10},{10,2},{3,11},{11,3},{32,40},{40,32... | collective-permute-start | bytes 479240 | tf_op jit(solution)/shard_map/ppermute | solution.py:47
  5.6 8.9 %collective-permute-start.1 = (bf16[208,384]{1,0:T(8,128)(2,1)}, bf16[208,384]{1,0:T(8,128)(2,1)S(1)}, u32[]{:S(2)}, u32[]{:S(2)}) collective-permute-start(bf16[208,384]{1,0:T(8,128)(2,1)} %get-tuple-element.36), channel_id=1, source_target_pairs={{0,32},{8,40},{1,33},{9,41},{2,34},{10,42},{3,35},{11,43},{32,64},... | collective-permute-start | bytes 479240 | tf_op jit(solution)/shard_map/ppermute | solution.py:47
  7.0 9.4 %collective-permute-start.2 = (bf16[208,384]{1,0:T(8,128)(2,1)}, bf16[208,384]{1,0:T(8,128)(2,1)S(1)}, u32[]{:S(2)}, u32[]{:S(2)}) collective-permute-start(bf16[208,384]{1,0:T(8,128)(2,1)} %get-tuple-element.37), channel_id=1, source_target_pairs={{0,40},{8,32},{1,41},{9,33},{2,42},{10,34},{3,43},{11,35},{32,72},... | collective-permute-start | bytes 479240 | tf_op jit(solution)/shard_map/ppermute | solution.py:47
  8.5 12.3 %collective-permute-start.3 = (bf16[208,384]{1,0:T(8,128)(2,1)}, bf16[208,384]{1,0:T(8,128)(2,1)S(1)}, u32[]{:S(2)}, u32[]{:S(2)}) collective-permute-start(bf16[208,384]{1,0:T(8,128)(2,1)} %get-tuple-element.38), channel_id=1, source_target_pairs={{0,64},{8,72},{1,65},{9,73},{2,66},{10,74},{3,67},{11,75},{32,96},... | collective-permute-start | bytes 479240 | tf_op jit(solution)/shard_map/ppermute | solution.py:47
  9.6 14.8 %collective-permute-start.4 = (bf16[208,384]{1,0:T(8,128)(2,1)}, bf16[208,384]{1,0:T(8,128)(2,1)S(1)}, u32[]{:S(2)}, u32[]{:S(2)}) collective-permute-start(bf16[208,384]{1,0:T(8,128)(2,1)} %get-tuple-element.39), channel_id=1, source_target_pairs={{0,72},{8,64},{1,73},{9,65},{2,74},{10,66},{3,75},{11,67},{32,104}... | collective-permute-start | bytes 479240 | tf_op jit(solution)/shard_map/ppermute | solution.py:47
  13.1 11.3 %collective-permute-start.5 = (bf16[208,384]{1,0:T(8,128)(2,1)}, bf16[208,384]{1,0:T(8,128)(2,1)S(1)}, u32[]{:S(2)}, u32[]{:S(2)}) collective-permute-start(bf16[208,384]{1,0:T(8,128)(2,1)} %get-tuple-element.40), channel_id=1, source_target_pairs={{0,96},{8,104},{1,97},{9,105},{2,98},{10,106},{3,99},{11,107},{32,... | collective-permute-start | bytes 479240 | tf_op jit(solution)/shard_map/ppermute | solution.py:47
  14.5 10.8 %collective-permute-start.6 = (bf16[208,384]{1,0:T(8,128)(2,1)}, bf16[208,384]{1,0:T(8,128)(2,1)S(1)}, u32[]{:S(2)}, u32[]{:S(2)}) collective-permute-start(bf16[208,384]{1,0:T(8,128)(2,1)} %get-tuple-element.41), channel_id=1, source_target_pairs={{0,104},{8,96},{1,105},{9,97},{2,106},{10,98},{3,107},{11,99},{32,... | collective-permute-start | bytes 479240 | tf_op jit(solution)/shard_map/ppermute | solution.py:47
  64.6 10.6 %collective-permute-start.7 = (bf16[8,16,128]{2,1,0:T(8,128)(2,1)}, bf16[8,16,128]{2,1,0:T(8,128)(2,1)S(1)}, u32[]{:S(2)}, u32[]{:S(2)}) collective-permute-start(bf16[8,16,128]{2,1,0:T(8,128)(2,1)} %get-tuple-element.42), channel_id=1, source_target_pairs={{0,16},{8,24},{1,17},{9,25},{2,18},{10,26},{3,19},{11,27},{32,48},... | collective-permute-start | bytes 98312 | tf_op jit(solution)/shard_map/ppermute | solution.py:47
  68.1 7.4 %collective-permute-start.10 = (bf16[1,8,64,128]{3,2,1,0:T(8,128)(2,1)}, bf16[1,8,64,128]{3,2,1,0:T(8,128)(2,1)S(1)}, u32[]{:S(2)}, u32[]{:S(2)}) collective-permute-start(bf16[1,8,64,128]{3,2,1,0:T(8,128)(2,1)} %get-tuple-element.43.refs_0_), channel_id=1, source_target_pairs={{0,20},{8,11},{1,21},{9,8},{2,22},{10,9},{3,23},{11,10},{32,52},{4... | collective-permute-start | bytes 393224 | tf_op jit(solution)/shard_map/ppermute | solution.py:47
  71.9 6.9 %collective-permute-start.8 = (bf16[1,8,64,128]{3,2,1,0:T(8,128)(2,1)}, bf16[1,8,64,128]{3,2,1,0:T(8,128)(2,1)S(1)}, u32[]{:S(2)}, u32[]{:S(2)}) collective-permute-start(bf16[1,8,64,128]{3,2,1,0:T(8,128)(2,1)} %get-tuple-element.43.refs_0_), channel_id=1, source_target_pairs={{0,4},{8,9},{1,5},{9,10},{2,6},{10,11},{3,7},{11,8},{32,36},{40,41... | collective-permute-start | bytes 393224 | tf_op jit(solution)/shard_map/ppermute | solution.py:47
  71.9 8.1 %collective-permute-start.9 = (bf16[1,8,64,128]{3,2,1,0:T(8,128)(2,1)}, bf16[1,8,64,128]{3,2,1,0:T(8,128)(2,1)S(1)}, u32[]{:S(2)}, u32[]{:S(2)}) collective-permute-start(bf16[1,8,64,128]{3,2,1,0:T(8,128)(2,1)} %get-tuple-element.43.refs_0_), channel_id=1, source_target_pairs={{0,16},{8,10},{1,17},{9,11},{2,18},{10,8},{3,19},{11,9},{32,48},{4... | collective-permute-start | bytes 393224 | tf_op jit(solution)/shard_map/ppermute | solution.py:47
  73.2 13.8 %collective-permute-start.17 = (bf16[2,8,64,128]{3,2,1,0:T(8,128)(2,1)}, bf16[2,8,64,128]{3,2,1,0:T(8,128)(2,1)S(1)}, u32[]{:S(2)}, u32[]{:S(2)}) collective-permute-start(bf16[2,8,64,128]{3,2,1,0:T(8,128)(2,1)} %get-tuple-element.49.refs_0_), channel_id=1, source_target_pairs={{0,4},{8,9},{1,5},{9,10},{2,6},{10,11},{3,7},{11,8},{32,36},{40,41... | collective-permute-start | bytes 786440 | tf_op jit(solution)/shard_map/ppermute | solution.py:47
  75.2 11.8 %collective-permute-start.11 = (bf16[1,2,8,64,128]{4,3,2,1,0:T(8,128)(2,1)}, bf16[1,2,8,64,128]{4,3,2,1,0:T(8,128)(2,1)S(1)}, u32[]{:S(2)}, u32[]{:S(2)}) collective-permute-start(bf16[1,2,8,64,128]{4,3,2,1,0:T(8,128)(2,1)} %get-tuple-element.44.refs_4_), channel_id=1, source_target_pairs={{0,1},{8,12},{1,2},{9,13},{2,3},{10,14},{3,0},{11,15},{32,33},{40,... | collective-permute-start | bytes 786440 | tf_op jit(solution)/shard_map/ppermute | solution.py:47
  75.6 14.6 %collective-permute-start.12 = (bf16[1,2,8,64,128]{4,3,2,1,0:T(8,128)(2,1)}, bf16[1,2,8,64,128]{4,3,2,1,0:T(8,128)(2,1)S(1)}, u32[]{:S(2)}, u32[]{:S(2)}) collective-permute-start(bf16[1,2,8,64,128]{4,3,2,1,0:T(8,128)(2,1)} %get-tuple-element.44.refs_4_), channel_id=1, source_target_pairs={{0,2},{8,24},{1,3},{9,25},{2,0},{10,26},{3,1},{11,27},{32,34},{40,... | collective-permute-start | bytes 786440 | tf_op jit(solution)/shard_map/ppermute | solution.py:47
  78.8 11.5 %collective-permute-start.13 = (bf16[1,2,8,64,128]{4,3,2,1,0:T(8,128)(2,1)}, bf16[1,2,8,64,128]{4,3,2,1,0:T(8,128)(2,1)S(1)}, u32[]{:S(2)}, u32[]{:S(2)}) collective-permute-start(bf16[1,2,8,64,128]{4,3,2,1,0:T(8,128)(2,1)} %get-tuple-element.44.refs_4_), channel_id=1, source_target_pairs={{0,3},{8,28},{1,0},{9,29},{2,1},{10,30},{3,2},{11,31},{32,35},{40,... | collective-permute-start | bytes 786440 | tf_op jit(solution)/shard_map/ppermute | solution.py:47
  80.0 26.0 %collective-permute-start.20 = (bf16[2,2,8,64,128]{4,3,2,1,0:T(8,128)(2,1)}, bf16[2,2,8,64,128]{4,3,2,1,0:T(8,128)(2,1)S(1)}, u32[]{:S(2)}, u32[]{:S(2)}) collective-permute-start(bf16[2,2,8,64,128]{4,3,2,1,0:T(8,128)(2,1)} %get-tuple-element.50.refs_4_), channel_id=1, source_target_pairs={{0,1},{8,12},{1,2},{9,13},{2,3},{10,14},{3,0},{11,15},{32,33},{40,... | collective-permute-start | bytes 1572872 | tf_op jit(solution)/shard_map/ppermute | solution.py:47
  87.0 19.0 %collective-permute-start.21 = (bf16[2,2,8,64,128]{4,3,2,1,0:T(8,128)(2,1)}, bf16[2,2,8,64,128]{4,3,2,1,0:T(8,128)(2,1)S(1)}, u32[]{:S(2)}, u32[]{:S(2)}) collective-permute-start(bf16[2,2,8,64,128]{4,3,2,1,0:T(8,128)(2,1)} %get-tuple-element.50.refs_4_), channel_id=1, source_target_pairs={{0,2},{8,24},{1,3},{9,25},{2,0},{10,26},{3,1},{11,27},{32,34},{40,... | collective-permute-start | bytes 1572872 | tf_op jit(solution)/shard_map/ppermute | solution.py:47
  87.0 20.2 %collective-permute-start.22 = (bf16[2,2,8,64,128]{4,3,2,1,0:T(8,128)(2,1)}, bf16[2,2,8,64,128]{4,3,2,1,0:T(8,128)(2,1)S(1)}, u32[]{:S(2)}, u32[]{:S(2)}) collective-permute-start(bf16[2,2,8,64,128]{4,3,2,1,0:T(8,128)(2,1)} %get-tuple-element.50.refs_4_), channel_id=1, source_target_pairs={{0,3},{8,28},{1,0},{9,29},{2,1},{10,30},{3,2},{11,31},{32,35},{40,... | collective-permute-start | bytes 1572872 | tf_op jit(solution)/shard_map/ppermute | solution.py:47
  90.2 12.5 %collective-permute-start.18 = (bf16[2,8,64,128]{3,2,1,0:T(8,128)(2,1)}, bf16[2,8,64,128]{3,2,1,0:T(8,128)(2,1)S(1)}, u32[]{:S(2)}, u32[]{:S(2)}) collective-permute-start(bf16[2,8,64,128]{3,2,1,0:T(8,128)(2,1)} %get-tuple-element.49.refs_0_), channel_id=1, source_target_pairs={{0,16},{8,10},{1,17},{9,11},{2,18},{10,8},{3,19},{11,9},{32,48},{4... | collective-permute-start | bytes 786440 | tf_op jit(solution)/shard_map/ppermute | solution.py:47
  90.3 15.7 %collective-permute-start.19 = (bf16[2,8,64,128]{3,2,1,0:T(8,128)(2,1)}, bf16[2,8,64,128]{3,2,1,0:T(8,128)(2,1)S(1)}, u32[]{:S(2)}, u32[]{:S(2)}) collective-permute-start(bf16[2,8,64,128]{3,2,1,0:T(8,128)(2,1)} %get-tuple-element.49.refs_0_), channel_id=1, source_target_pairs={{0,20},{8,11},{1,21},{9,8},{2,22},{10,9},{3,23},{11,10},{32,52},{4... | collective-permute-start | bytes 786440 | tf_op jit(solution)/shard_map/ppermute | solution.py:47
  102.8 28.4 %collective-permute-start.14 = (bf16[544,128]{1,0:T(8,128)(2,1)}, bf16[544,128]{1,0:T(8,128)(2,1)S(1)}, u32[]{:S(2)}, u32[]{:S(2)}) collective-permute-start(bf16[544,128]{1,0:T(8,128)(2,1)} %get-tuple-element.46), channel_id=1, source_target_pairs={{0,20},{8,11},{1,21},{9,8},{2,22},{10,9},{3,23},{11,10},{32,52},{4... | collective-permute-start | bytes 417800 | tf_op jit(solution)/shard_map/ppermute | solution.py:47
  126.1 14.9 %collective-permute-start.23 = (bf16[1088,128]{1,0:T(8,128)(2,1)}, bf16[1088,128]{1,0:T(8,128)(2,1)S(1)}, u32[]{:S(2)}, u32[]{:S(2)}) collective-permute-start(bf16[1088,128]{1,0:T(8,128)(2,1)} %get-tuple-element.52), channel_id=1, source_target_pairs={{0,20},{8,11},{1,21},{9,8},{2,22},{10,9},{3,23},{11,10},{32,52},{4... | collective-permute-start | bytes 835592 | tf_op jit(solution)/shard_map/ppermute | solution.py:47
  128.0 13.1 %collective-permute-start.24 = (bf16[1088,128]{1,0:T(8,128)(2,1)}, bf16[1088,128]{1,0:T(8,128)(2,1)S(1)}, u32[]{:S(2)}, u32[]{:S(2)}) collective-permute-start(bf16[1088,128]{1,0:T(8,128)(2,1)} %get-tuple-element.53), channel_id=1, source_target_pairs={{0,16},{8,10},{1,17},{9,11},{2,18},{10,8},{3,19},{11,9},{32,48},{4... | collective-permute-start | bytes 835592 | tf_op jit(solution)/shard_map/ppermute | solution.py:47
  128.0 13.1 %collective-permute-start.25 = (bf16[1088,128]{1,0:T(8,128)(2,1)}, bf16[1088,128]{1,0:T(8,128)(2,1)S(1)}, u32[]{:S(2)}, u32[]{:S(2)}) collective-permute-start(bf16[1088,128]{1,0:T(8,128)(2,1)} %get-tuple-element.54), channel_id=1, source_target_pairs={{0,4},{8,9},{1,5},{9,10},{2,6},{10,11},{3,7},{11,8},{32,36},{40,41... | collective-permute-start | bytes 835592 | tf_op jit(solution)/shard_map/ppermute | solution.py:47
  128.6 11.1 %collective-permute-start.15 = (bf16[544,128]{1,0:T(8,128)(2,1)S(1)}, bf16[544,128]{1,0:T(8,128)(2,1)S(1)}, u32[]{:S(2)}, u32[]{:S(2)}) collective-permute-start(bf16[544,128]{1,0:T(8,128)(2,1)S(1)} %copy-done.35), channel_id=1, source_target_pairs={{0,16},{8,10},{1,17},{9,11},{2,18},{10,8},{3,19},{11,9},{32,48},{4... | collective-permute-start | bytes 417800 | tf_op jit(solution)/shard_map/ppermute | solution.py:47
  131.2 9.8 %collective-permute-start.16 = (bf16[544,128]{1,0:T(8,128)(2,1)S(1)}, bf16[544,128]{1,0:T(8,128)(2,1)S(1)}, u32[]{:S(2)}, u32[]{:S(2)}) collective-permute-start(bf16[544,128]{1,0:T(8,128)(2,1)S(1)} %copy-done.34), channel_id=1, source_target_pairs={{0,4},{8,9},{1,5},{9,10},{2,6},{10,11},{3,7},{11,8},{32,36},{40,41... | collective-permute-start | bytes 417800 | tf_op jit(solution)/shard_map/ppermute | solution.py:47
  145.9 9.5 %collective-permute-start.26 = (bf16[64,384]{1,0:T(8,128)(2,1)}, bf16[64,384]{1,0:T(8,128)(2,1)S(1)}, u32[]{:S(2)}, u32[]{:S(2)}) collective-permute-start(bf16[64,384]{1,0:T(8,128)(2,1)} %get-tuple-element.56), channel_id=1, source_target_pairs={{0,8},{8,0},{1,9},{9,1},{2,10},{10,2},{3,11},{11,3},{32,40},{40,32... | collective-permute-start | bytes 147464 | tf_op jit(solution)/shard_map/ppermute | solution.py:47
  148.9 7.8 %collective-permute-start.27 = (bf16[64,384]{1,0:T(8,128)(2,1)}, bf16[64,384]{1,0:T(8,128)(2,1)S(1)}, u32[]{:S(2)}, u32[]{:S(2)}) collective-permute-start(bf16[64,384]{1,0:T(8,128)(2,1)} %get-tuple-element.57), channel_id=1, source_target_pairs={{0,96},{8,104},{1,97},{9,105},{2,98},{10,106},{3,99},{11,107},{32,... | collective-permute-start | bytes 147464 | tf_op jit(solution)/shard_map/ppermute | solution.py:47
  151.7 5.7 %collective-permute-start.28 = (bf16[64,384]{1,0:T(8,128)(2,1)}, bf16[64,384]{1,0:T(8,128)(2,1)S(1)}, u32[]{:S(2)}, u32[]{:S(2)}) collective-permute-start(bf16[64,384]{1,0:T(8,128)(2,1)} %get-tuple-element.58), channel_id=1, source_target_pairs={{0,104},{8,96},{1,105},{9,97},{2,106},{10,98},{3,107},{11,99},{32,... | collective-permute-start | bytes 147464 | tf_op jit(solution)/shard_map/ppermute | solution.py:47
  152.0 5.4 %collective-permute-start.29 = (bf16[64,384]{1,0:T(8,128)(2,1)}, bf16[64,384]{1,0:T(8,128)(2,1)S(1)}, u32[]{:S(2)}, u32[]{:S(2)}) collective-permute-start(bf16[64,384]{1,0:T(8,128)(2,1)} %get-tuple-element.59), channel_id=1, source_target_pairs={{0,64},{8,72},{1,65},{9,73},{2,66},{10,74},{3,67},{11,75},{32,96},... | collective-permute-start | bytes 147464 | tf_op jit(solution)/shard_map/ppermute | solution.py:47
  153.1 5.9 %collective-permute-start.30 = (bf16[64,384]{1,0:T(8,128)(2,1)}, bf16[64,384]{1,0:T(8,128)(2,1)S(1)}, u32[]{:S(2)}, u32[]{:S(2)}) collective-permute-start(bf16[64,384]{1,0:T(8,128)(2,1)} %get-tuple-element.60), channel_id=1, source_target_pairs={{0,72},{8,64},{1,73},{9,65},{2,74},{10,66},{3,75},{11,67},{32,104}... | collective-permute-start | bytes 147464 | tf_op jit(solution)/shard_map/ppermute | solution.py:47
  156.7 5.1 %collective-permute-start.32 = (bf16[64,384]{1,0:T(8,128)(2,1)}, bf16[64,384]{1,0:T(8,128)(2,1)S(1)}, u32[]{:S(2)}, u32[]{:S(2)}) collective-permute-start(bf16[64,384]{1,0:T(8,128)(2,1)} %get-tuple-element.62), channel_id=1, source_target_pairs={{0,40},{8,32},{1,41},{9,33},{2,42},{10,34},{3,43},{11,35},{32,72},... | collective-permute-start | bytes 147464 | tf_op jit(solution)/shard_map/ppermute | solution.py:47
  (38 other events, 218.4 us)
